TPU v7x, 256 devices: a whole 4x4x8 slice. The times are simulated.
256 devices in a mesh: mp: 2 (over z_hi), dp: 8 (over y, core), tensor: 16 (over z_lo, x).
Axes of the slice: x: 4, y: 4, z: 8 (z_hi: 2, z_lo: 4; z = z_hi * 4 + z_lo), core: 2. Of those that a mesh axis runs over, the one named last changes fastest.
Arguments:
- activations: bfloat16 [2, 1024, 8192], P('mp', 'dp'), may hold values from -6 to 6
- gate_pre: bfloat16 [2, 1024, 28672], P('mp', 'dp', 'tensor'), may hold values from -6 to 6
- hidden_grad: bfloat16 [2, 1024, 28672], P('mp', 'dp', 'tensor'), may hold values from -1.2 to 1.2, as said below
- up_weights: bfloat16 [2, 8192, 28672], P('mp', 'dp', 'tensor'), may hold values from -6 to 6
Outputs:
- merged: bfloat16 [8192, 28672], P(('dp', 'mp'), 'tensor')
Inputs may be any that keep to these rules, and one draw needn't show every extreme that they name: `hidden_grad`: each sequence's values share one scale, spread evenly in the logarithm between 0.005 and 0.3 over sequences.
All inputs are finite; a program needn't handle non-finite values.
Results may differ from a plain program's by a relative error of at most 0.003.
Values may be sent and summed in bfloat16 or wider, within the bound.
No kernel may reach another device: no remote copies, remote signals or barrier semaphores. Data moves between devices by JAX's collectives and lax.ppermute only.
A program may use at most 192 MiB of HBM per device.

v0:
```python
import math

import jax
import jax.numpy as jnp
from jax import lax
from jax.sharding import PartitionSpec as P

D = 8192
FF = 28672
LEN = 128


clip_ratio = 0.05
fisher_floor = 0.1


def from_everyone(value, axis):
    length = lax.axis_size(axis)
    return lax.all_to_all(
        jnp.broadcast_to(value[None], (length, *value.shape)), axis, 0, 0, tiled=True
    )


def of_everyone(value, axis):
    everything = from_everyone(value, axis)
    return jnp.sum(everything, axis=0)


def split_up(value, dim, length):
    lengths = value.shape
    parts = value.reshape(*lengths[:dim], length, lengths[dim] // length, *lengths[dim + 1 :])
    return jnp.moveaxis(parts, dim, 0)


def edges_of(length, count):
    unit = 8 if length >= 8 * count else 1
    return [length // unit * k // count * unit for k in range(1, count)]


def in_order(parts, dim):
    lengths = list(parts.shape[1:])
    lengths[dim] *= parts.shape[0]
    return jnp.moveaxis(parts, 0, dim).reshape(lengths)


def several_exchanges(value, axis, pieces, split_dim, concat_dim):
    parts = split_up(value, split_dim, lax.axis_size(axis))
    split_at = max(range(1, max(2, parts.ndim - 1)), key=lambda d: parts.shape[d])
    done = []
    for section in jnp.split(parts, edges_of(parts.shape[split_at], pieces), axis=split_at):
        if section.size:
            done.append(lax.all_to_all(section, axis, split_axis=0, concat_axis=0, tiled=True))
    return in_order(jnp.concatenate(done, axis=split_at), concat_dim)


def collect(value, axis, dim):
    return in_order(from_everyone(value, axis), dim)


def for_sending(value):

    def short(part):
        return part.astype(jnp.bfloat16) if part.dtype == jnp.float32 else part

    return jax.tree.map(short, value)


def local(activations, gate_pre, hidden_grad, up_weights):
    single_precision = jnp.float32
    input_row_block = activations[0]
    tokens_per_worker, width = input_row_block.shape
    seq_dev = tokens_per_worker // LEN
    cot = (
        hidden_grad[0].astype(single_precision) * jax.nn.silu(gate_pre[0].astype(single_precision))
    ).astype(jnp.bfloat16)
    cot_seq = cot.reshape(seq_dev, LEN, cot.shape[1])
    sequence_inputs = input_row_block.reshape(seq_dev, LEN, width)
    input_gram_matrix = jnp.einsum(
        "tpe,txe->tpx", sequence_inputs, sequence_inputs, preferred_element_type=single_precision
    )
    gram_local = jnp.einsum(
        "slf,smf->slm", cot_seq, cot_seq, preferred_element_type=single_precision
    )
    gram_cot = of_everyone(gram_local, "tensor")
    grad_norm = jnp.sqrt(jnp.sum(input_gram_matrix * gram_cot, axis=(1, 2)))
    clip_limit = clip_ratio * math.sqrt(LEN * D * FF)
    factor = clip_limit / jnp.maximum(grad_norm, clip_limit)
    clip_sq = factor * factor
    row_block = lax.all_to_all(input_row_block, "dp", split_axis=1, concat_axis=0, tiled=True)
    both_acts = lax.all_to_all(row_block[None], "mp", split_axis=2, concat_axis=0, tiled=True)
    both_weights = several_exchanges(up_weights, "mp", 2, 1, 0)
    both_cot, both_clip = (
        collect(cot_seq[None], "mp", 0),
        collect(clip_sq[None].astype(jnp.bfloat16), "mp", 0).astype(jnp.float32),
    )
    model_total_count = both_acts.shape[0]
    acts_models = both_acts.reshape(model_total_count, -1, LEN, both_acts.shape[2])
    start_both = jnp.zeros(both_weights.shape, single_precision)
    cot_piece = lax.all_gather(both_cot, "dp", axis=1, tiled=True)
    scale_piece = lax.all_gather(for_sending(both_clip), "dp", axis=1, tiled=True)
    count = cot_piece.shape[1]

    def one_seq(seq_index, total):
        grad = jnp.einsum(
            "mld,mlf->mdf",
            acts_models[:, seq_index],
            cot_piece[:, seq_index],
            preferred_element_type=single_precision,
        )
        return total + scale_piece[:, seq_index, None, None] * grad * grad

    fisher_both = lax.fori_loop(0, count, one_seq, start_both)
    weighted = fisher_both + fisher_floor
    numer = jnp.sum(weighted * both_weights.astype(single_precision), axis=0)
    denom = jnp.sum(weighted, axis=0)
    return (numer / denom).astype(jnp.bfloat16)


def solution(mesh):
    placed = (
        P("mp", "dp", None),
        P("mp", "dp", "tensor"),
        P("mp", "dp", "tensor"),
        P("mp", "dp", "tensor"),
    )
    return jax.shard_map(
        local, mesh=mesh, in_specs=placed, out_specs=P(("dp", "mp"), "tensor"), check_vma=False
    )
```

profile of v0, /device:TPU:38, one launch (start us, length us, event | category | flops | bytes accessed | tf_op | source)
XLA Modules:
  0.0 317.1 jit_solution(6462977133960851835)
XLA Ops:
  8.2 33.3 %all_to_all.56 = bf16[2,1,1,128,1792]{4,3,1,2,0:T(8,128)(2,1)} all-to-all(bf16[2,1,1,128,1792]{4,3,1,2,0:T(8,128)(2,1)S(1)} %broadcast_in_dim.28), channel_id=1, replica_groups=mesh['mp'=2,'dp'=8,'tensor'=16] {'mp'}, dimensions={0} | all-to-all | bytes 1835008 | tf_op jit(solution)/shard_map/all_to_all | solution.py:19
  44.0 4.5 %all-to-all-start.2 = ((bf16[128,8,1024]{0,2,1:T(8,128)(2,1)}), bf16[128,8,1024]{0,2,1:T(8,128)(2,1)S(1)}, u32[]{:S(2)}, u32[]{:S(2)}) async-start(bf16[128,8,1024]{0,2,1:T(8,128)(2,1)} %bitcast.71), calls=%async_computation.2 | async-start | bytes 4194304 | tf_op jit(solution)/shard_map/all_to_all | solution.py:89
  49.2 46.4 %all-to-all-done.2 = bf16[128,8,1024]{0,2,1:T(8,128)(2,1)S(1)} async-done(((bf16[128,8,1024]{0,2,1:T(8,128)(2,1)}), bf16[128,8,1024]{0,2,1:T(8,128)(2,1)S(1)}, u32[]{:S(2)}, u32[]{:S(2)}) %all-to-all-start.2) | async-done | bytes 2097184 | tf_op jit(solution)/shard_map/all_to_all | solution.py:89
  96.7 5.8 %all-to-all-start = ((f32[16,1,128,128]{3,2,1,0:T(8,128)}), f32[16,1,128,128]{3,2,1,0:T(8,128)S(1)}, u32[]{:S(2)}, u32[]{:S(2)}) async-start(f32[16,1,128,128]{3,2,1,0:T(8,128)} %broadcast_in_dim.11), calls=%async_computation | async-start | bytes 2097152 | tf_op jit(solution)/shard_map/all_to_all | solution.py:19
  105.4 7.8 %copy.35 = bf16[1,1024,1024]{1,0,2:T(2,128)(2,1)} copy(bf16[1,1024,1024]{2,1,0:T(8,128)(2,1)S(1)} %bitcast.68) | data formatting | bytes 4194304 | tf_op jit(solution)/shard_map/broadcast_in_dim | solution.py:90
  113.6 12.7 %reduce.3 = bf16[1024,1024]{1,0:T(8,128)(2,1)S(1)} reduce(bf16[1024,1,1024]{2,1,0:T(2,128)(2,1)} %bitcast.66, bf16[]{:T(256)} %broadcast.23), dimensions={1}, to_apply=%bitcast.58.reduce_sub_computation | reduce | bytes 4194306
  133.3 10.0 %all_to_all.57 = bf16[2,1,1]{1,2,0:T(2,128)(2,1)S(1)} all-to-all(bf16[2,1,1]{1,2,0:T(2,128)(2,1)S(1)} %broadcast_in_dim.12), channel_id=1, replica_groups=mesh['mp'=2,'dp'=8,'tensor'=16] {'mp'}, dimensions={0} | all-to-all | bytes 8 | tf_op jit(solution)/shard_map/all_to_all | solution.py:19
  143.3 3.8 %all-to-all-start.3 = ((bf16[2,2,262144]{2,1,0:T(2,128)(2,1)}), bf16[2,2,262144]{2,1,0:T(2,128)(2,1)S(1)}, u32[]{:S(2)}, u32[]{:S(2)}) async-start(bf16[2,2,262144]{2,1,0:T(2,128)(2,1)} %reshape.97), calls=%async_computation.3 | async-start | bytes 4194304 | tf_op jit(solution)/shard_map/all_to_all | solution.py:90
  147.0 4.2 %fusion.30 = (bf16[2,1,256,1792]{3,2,1,0:T(8,128)(2,1)}, bf16[2,1,256,1792]{3,2,1,0:T(8,128)(2,1)}) fusion(bf16[2,1,512,1792]{3,2,1,0:T(8,128)(2,1)} %bitcast.73), kind=kLoop, calls=%fused_computation.37 | loop fusion | bytes 7340032 | tf_op jit(solution)/shard_map/split | solution.py:50
  151.2 44.1 %all-to-all-done.3 = bf16[2,2,262144]{2,1,0:T(2,128)(2,1)S(1)} async-done(((bf16[2,2,262144]{2,1,0:T(2,128)(2,1)}), bf16[2,2,262144]{2,1,0:T(2,128)(2,1)S(1)}, u32[]{:S(2)}, u32[]{:S(2)}) %all-to-all-start.3) | async-done | bytes 2097184 | tf_op jit(solution)/shard_map/all_to_all | solution.py:90
  195.3 4.7 %all-to-all-start.6 = ((bf16[2,1,256,1792]{3,2,1,0:T(8,128)(2,1)}), bf16[2,1,256,1792]{3,2,1,0:T(8,128)(2,1)}, u32[]{:S(2)}, u32[]{:S(2)}) async-start(bf16[2,1,256,1792]{3,2,1,0:T(8,128)(2,1)} %get-tuple-element.161), calls=%async_computation.6 | async-start | bytes 3670016 | tf_op jit(solution)/shard_map/all_to_all | solution.py:52
  200.2 8.4 %all-gather = bf16[2,8,1]{2,0,1:T(2,128)(2,1)S(1)} all-gather(bf16[2,1,1]{2,0,1:T(2,128)(2,1)S(1)} %copy.31), channel_id=2, replica_groups=mesh['mp'=2,'dp'=8,'tensor'=16] {'dp'}, dimensions={1}, use_global_device_ids=true | all-gather | bytes 36 | tf_op jit(solution)/shard_map/all_gather | solution.py:100
  217.4 19.3 %all-to-all-done.6 = bf16[2,1,256,1792]{3,2,1,0:T(8,128)(2,1)} async-done(((bf16[2,1,256,1792]{3,2,1,0:T(8,128)(2,1)}), bf16[2,1,256,1792]{3,2,1,0:T(8,128)(2,1)}, u32[]{:S(2)}, u32[]{:S(2)}) %all-to-all-start.6) | async-done | bytes 1835040 | tf_op jit(solution)/shard_map/all_to_all | solution.py:52
  236.6 5.5 %all-to-all-start.5 = ((bf16[2,1,256,1792]{3,2,1,0:T(8,128)(2,1)}), bf16[2,1,256,1792]{3,2,1,0:T(8,128)(2,1)S(1)}, u32[]{:S(2)}, u32[]{:S(2)}) async-start(bf16[2,1,256,1792]{3,2,1,0:T(8,128)(2,1)} %get-tuple-element.160), calls=%async_computation.5 | async-start | bytes 3670016 | tf_op jit(solution)/shard_map/all_to_all | solution.py:52
  242.1 61.3 %while.14 = (s32[]{:T(128)}, f32[2,512,1792]{2,1,0:T(8,128)}, bf16[2,8]{1,0:T(2,128)(2,1)S(1)}, bf16[2,8,128,512]{3,2,1,0:T(8,128)(2,1)}, bf16[2,8,128,1792]{3,2,0,1:T(8,128)(2,1)}, /*index=5*/s32[]{:T(128)}, s32[]{:T(128)}) while((s32[]{:T(128)}, f32[2,512,1792]{2,1,0:T(8,128)}, bf16[2,8]{1,0:T(2,128)(2,1)S(1)}, ...), condition=%wide.region_3.4_spmd.clone, body=%wide.region_2.3_spmd.clone.sunk | while | flops 477102080 | bytes 15861382 | solution.py:112
  242.3 5.6 %fusion.36 = f32[2,512,1792]{2,1,0:T(8,128)} fusion(f32[2,512,1792]{2,1,0:T(8,128)} %get-tuple-element.201, f32[2]{0:T(128)S(1)} %bitcast_convert_fusion.2, pred[]{:T(512)S(6)} %compare.3, bf16[2,8,128,1792]{3,2,0,1:T(8,128)(2,1)} %get-tuple-element.211, s32[]{:T(128)S(6)} %copy.47, bf16[2,8,128,512]{3,2,1,0:T(8,128)(2,1)} %get-tuple-element.210), kind=kOutput, calls=%fused_computation.1.clone.1 | convolution fusion | flops 477102080 | bytes 15861256 | tf_op jit(solution)/shard_map/while/body/eval_jaxpr/mld,mlf->mdf/dot_general | solution.py:104
  248.1 7.7 %fusion.36 = f32[2,512,1792]{2,1,0:T(8,128)} fusion(f32[2,512,1792]{2,1,0:T(8,128)} %get-tuple-element.201, f32[2]{0:T(128)S(1)} %bitcast_convert_fusion.2, pred[]{:T(512)S(6)} %compare.3, bf16[2,8,128,1792]{3,2,0,1:T(8,128)(2,1)} %get-tuple-element.211, s32[]{:T(128)S(6)} %copy.47, bf16[2,8,128,512]{3,2,1,0:T(8,128)(2,1)} %get-tuple-element.210), kind=kOutput, calls=%fused_computation.1.clone.1 | convolution fusion | flops 477102080 | bytes 15861256 | tf_op jit(solution)/shard_map/while/body/eval_jaxpr/mld,mlf->mdf/dot_general | solution.py:104
  256.0 7.7 %fusion.36 = f32[2,512,1792]{2,1,0:T(8,128)} fusion(f32[2,512,1792]{2,1,0:T(8,128)} %get-tuple-element.201, f32[2]{0:T(128)S(1)} %bitcast_convert_fusion.2, pred[]{:T(512)S(6)} %compare.3, bf16[2,8,128,1792]{3,2,0,1:T(8,128)(2,1)} %get-tuple-element.211, s32[]{:T(128)S(6)} %copy.47, bf16[2,8,128,512]{3,2,1,0:T(8,128)(2,1)} %get-tuple-element.210), kind=kOutput, calls=%fused_computation.1.clone.1 | convolution fusion | flops 477102080 | bytes 15861256 | tf_op jit(solution)/shard_map/while/body/eval_jaxpr/mld,mlf->mdf/dot_general | solution.py:104
  263.9 7.7 %fusion.36 = f32[2,512,1792]{2,1,0:T(8,128)} fusion(f32[2,512,1792]{2,1,0:T(8,128)} %get-tuple-element.201, f32[2]{0:T(128)S(1)} %bitcast_convert_fusion.2, pred[]{:T(512)S(6)} %compare.3, bf16[2,8,128,1792]{3,2,0,1:T(8,128)(2,1)} %get-tuple-element.211, s32[]{:T(128)S(6)} %copy.47, bf16[2,8,128,512]{3,2,1,0:T(8,128)(2,1)} %get-tuple-element.210), kind=kOutput, calls=%fused_computation.1.clone.1 | convolution fusion | flops 477102080 | bytes 15861256 | tf_op jit(solution)/shard_map/while/body/eval_jaxpr/mld,mlf->mdf/dot_general | solution.py:104
  271.9 7.7 %fusion.36 = f32[2,512,1792]{2,1,0:T(8,128)} fusion(f32[2,512,1792]{2,1,0:T(8,128)} %get-tuple-element.201, f32[2]{0:T(128)S(1)} %bitcast_convert_fusion.2, pred[]{:T(512)S(6)} %compare.3, bf16[2,8,128,1792]{3,2,0,1:T(8,128)(2,1)} %get-tuple-element.211, s32[]{:T(128)S(6)} %copy.47, bf16[2,8,128,512]{3,2,1,0:T(8,128)(2,1)} %get-tuple-element.210), kind=kOutput, calls=%fused_computation.1.clone.1 | convolution fusion | flops 477102080 | bytes 15861256 | tf_op jit(solution)/shard_map/while/body/eval_jaxpr/mld,mlf->mdf/dot_general | solution.py:104
  279.8 7.7 %fusion.36 = f32[2,512,1792]{2,1,0:T(8,128)} fusion(f32[2,512,1792]{2,1,0:T(8,128)} %get-tuple-element.201, f32[2]{0:T(128)S(1)} %bitcast_convert_fusion.2, pred[]{:T(512)S(6)} %compare.3, bf16[2,8,128,1792]{3,2,0,1:T(8,128)(2,1)} %get-tuple-element.211, s32[]{:T(128)S(6)} %copy.47, bf16[2,8,128,512]{3,2,1,0:T(8,128)(2,1)} %get-tuple-element.210), kind=kOutput, calls=%fused_computation.1.clone.1 | convolution fusion | flops 477102080 | bytes 15861256 | tf_op jit(solution)/shard_map/while/body/eval_jaxpr/mld,mlf->mdf/dot_general | solution.py:104
  287.8 7.7 %fusion.36 = f32[2,512,1792]{2,1,0:T(8,128)} fusion(f32[2,512,1792]{2,1,0:T(8,128)} %get-tuple-element.201, f32[2]{0:T(128)S(1)} %bitcast_convert_fusion.2, pred[]{:T(512)S(6)} %compare.3, bf16[2,8,128,1792]{3,2,0,1:T(8,128)(2,1)} %get-tuple-element.211, s32[]{:T(128)S(6)} %copy.47, bf16[2,8,128,512]{3,2,1,0:T(8,128)(2,1)} %get-tuple-element.210), kind=kOutput, calls=%fused_computation.1.clone.1 | convolution fusion | flops 477102080 | bytes 15861256 | tf_op jit(solution)/shard_map/while/body/eval_jaxpr/mld,mlf->mdf/dot_general | solution.py:104
  295.7 7.7 %fusion.36 = f32[2,512,1792]{2,1,0:T(8,128)} fusion(f32[2,512,1792]{2,1,0:T(8,128)} %get-tuple-element.201, f32[2]{0:T(128)S(1)} %bitcast_convert_fusion.2, pred[]{:T(512)S(6)} %compare.3, bf16[2,8,128,1792]{3,2,0,1:T(8,128)(2,1)} %get-tuple-element.211, s32[]{:T(128)S(6)} %copy.47, bf16[2,8,128,512]{3,2,1,0:T(8,128)(2,1)} %get-tuple-element.210), kind=kOutput, calls=%fused_computation.1.clone.1 | convolution fusion | flops 477102080 | bytes 15861256 | tf_op jit(solution)/shard_map/while/body/eval_jaxpr/mld,mlf->mdf/dot_general | solution.py:104
  303.4 5.1 %add_reduce_fusion = (f32[512,1792]{1,0:T(8,128)S(1)}, f32[512,1792]{1,0:T(8,128)S(1)}) fusion(f32[2,512,1792]{2,1,0:T(8,128)} %get-tuple-element.99, bf16[2,1,256,1792]{3,2,1,0:T(8,128)(2,1)} %all-to-all-done.6, bf16[2,1,256,1792]{3,2,1,0:T(8,128)(2,1)S(1)} %all-to-all-done.5), kind=kLoop, calls=%fused_computation.11 | loop fusion | flops 14680064 | bytes 18350080 | tf_op jit(solution)/shard_map/reduce_sum | solution.py:115
  (55 shorter events, 27.6 us)
Async XLA Ops:
  6.5 35.0 %copy-start.1 = (bf16[1,128,8192]{2,1,0:T(8,128)(2,1)S(1)}, bf16[1,128,8192]{2,1,0:T(8,128)(2,1)}, u32[]{:S(2)}) copy-start(bf16[1,128,8192]{2,1,0:T(8,128)(2,1)} %param.6) | copy-start | bytes 6291460
  6.5 235.6 %all-gather.4.cloned.1.call-start = ((), (), s32[]{:S(2)}) async-start(), calls=%async_computation.7 | async-start | bytes 8257536 | tf_op jit(solution)/shard_map/all_gather | solution.py:99
  41.5 7.0 %copy-start.2 = (bf16[1,128,1792]{2,1,0:T(8,128)(2,1)S(1)}, bf16[1,128,1792]{2,1,0:T(8,128)(2,1)}, u32[]{:S(2)}) copy-start(bf16[1,128,1792]{2,1,0:T(8,128)(2,1)} %param.8) | copy-start | bytes 1376260
  41.5 7.0 %copy-start.3 = (bf16[1,128,1792]{2,1,0:T(8,128)(2,1)S(1)}, bf16[1,128,1792]{2,1,0:T(8,128)(2,1)}, u32[]{:S(2)}) copy-start(bf16[1,128,1792]{2,1,0:T(8,128)(2,1)} %param.7) | copy-start | bytes 1376260
  44.0 51.5 %all-to-all-start.2 = ((bf16[128,8,1024]{0,2,1:T(8,128)(2,1)}), bf16[128,8,1024]{0,2,1:T(8,128)(2,1)S(1)}, u32[]{:S(2)}, u32[]{:S(2)}) async-start(bf16[128,8,1024]{0,2,1:T(8,128)(2,1)} %bitcast.71), calls=%async_computation.2 | async-start | bytes 4194304 | tf_op jit(solution)/shard_map/all_to_all | solution.py:89
  95.5 7.0 %copy-start = (bf16[128,8,1024]{0,2,1:T(8,128)(2,1)}, bf16[128,8,1024]{0,2,1:T(8,128)(2,1)S(1)}, u32[]{:S(2)}) copy-start(bf16[128,8,1024]{0,2,1:T(8,128)(2,1)S(1)} %all-to-all-done.2) | copy-start | bytes 6291460
  96.7 32.2 %all-to-all-start = ((f32[16,1,128,128]{3,2,1,0:T(8,128)}), f32[16,1,128,128]{3,2,1,0:T(8,128)S(1)}, u32[]{:S(2)}, u32[]{:S(2)}) async-start(f32[16,1,128,128]{3,2,1,0:T(8,128)} %broadcast_in_dim.11), calls=%async_computation | async-start | bytes 2097152 | tf_op jit(solution)/shard_map/all_to_all | solution.py:19
  143.3 52.0 %all-to-all-start.3 = ((bf16[2,2,262144]{2,1,0:T(2,128)(2,1)}), bf16[2,2,262144]{2,1,0:T(2,128)(2,1)S(1)}, u32[]{:S(2)}, u32[]{:S(2)}) async-start(bf16[2,2,262144]{2,1,0:T(2,128)(2,1)} %reshape.97), calls=%async_computation.3 | async-start | bytes 4194304 | tf_op jit(solution)/shard_map/all_to_all | solution.py:90
  195.3 41.3 %all-to-all-start.6 = ((bf16[2,1,256,1792]{3,2,1,0:T(8,128)(2,1)}), bf16[2,1,256,1792]{3,2,1,0:T(8,128)(2,1)}, u32[]{:S(2)}, u32[]{:S(2)}) async-start(bf16[2,1,256,1792]{3,2,1,0:T(8,128)(2,1)} %get-tuple-element.161), calls=%async_computation.6 | async-start | bytes 3670016 | tf_op jit(solution)/shard_map/all_to_all | solution.py:52
  236.6 66.8 %all-to-all-start.5 = ((bf16[2,1,256,1792]{3,2,1,0:T(8,128)(2,1)}), bf16[2,1,256,1792]{3,2,1,0:T(8,128)(2,1)S(1)}, u32[]{:S(2)}, u32[]{:S(2)}) async-start(bf16[2,1,256,1792]{3,2,1,0:T(8,128)(2,1)} %get-tuple-element.160), calls=%async_computation.5 | async-start | bytes 3670016 | tf_op jit(solution)/shard_map/all_to_all | solution.py:52
Sparse Core Ops, SparseCore 0:
  41.6 64.9 all-gather.3
where the time goes:
time: 318 us; the launch traced here: 317 us
  waiting for transfers between devices  110 us (35%)
  matrix products  63.9 us (20%)
  blocking collectives  51.7 us (16%)
  local copies, waits for them, and re-layouts  31.9 us (10%)
  starting transfers between devices  24.3 us (8%)
  other arithmetic  21.2 us (7%)
  between operations  14.3 us (4%)
    dot_general x8, matrix products, one_seq(): jnp.einsum('mld,mlf->mdf', acts_models[:, seq_index], cot_piece[:, seq_in...  59.8 us
    all_to_all x1, waiting for transfers between devices, local(): lax.all_to_all(input_row_block, 'dp', split_axis=1, concat_axis=0, tiled=...  46.4 us
    all_to_all x1, waiting for transfers between devices, local(): lax.all_to_all(row_block[None], 'mp', split_axis=2, concat_axis=0, tiled=...  44.1 us
    all_to_all x2, blocking collectives, from_everyone(): lax.all_to_all(jnp.broadcast_to(value[None], (length, *value.shape)), axi...  43.3 us
    all_to_all x2, waiting for transfers between devices, several_exchanges(): lax.all_to_all(section, axis, split_axis=0, concat_axis=0, tiled=True)  19.3 us
    unnamed x2, other arithmetic  12.7 us
    unnamed x13, local copies, waits for them, and re-layouts  11.7 us
    all_to_all x2, starting transfers between devices, several_exchanges(): lax.all_to_all(section, axis, split_axis=0, concat_axis=0, tiled=True)  10.2 us
  transfers between devices with their start and end apart: 6, of which 3 were waited for; matrix products, arithmetic and copies ran while one was open for 34% of the time, Pallas kernels for 0%

commit v1 on v0

v1 whole, which is shorter than its diff:
```python
import functools
import math

import jax
import jax.numpy as jnp
from jax import lax
from jax.experimental import pallas as pl
from jax.experimental.pallas import tpu as pltpu
from jax.sharding import PartitionSpec as P


D = 8192
FF = 28672
LEN = 128
CLIP_RATIO = 0.05
FLOOR = 0.1

N_Y, N_CORE, N_Z, N_X = 4, 2, 4, 4
N_DP = N_Y * N_CORE
N_TENSOR = N_Z * N_X
N_MP = 2
MP_SWAP = [(0, 1), (1, 0)]
CORE_SWAP = [(i, i ^ 1) for i in range(N_DP)]
VMEM_LIMIT = 50 * 1024 * 1024


def exchange(value, axis):
    return lax.all_to_all(value, axis, 0, 0, tiled=True)


def y_shift(k):
    return [
        (y * N_CORE + c, (y + k) % N_Y * N_CORE + c) for y in range(N_Y) for c in range(N_CORE)
    ]


def x_shift(k):
    return [(z * N_X + x, z * N_X + (x + k) % N_X) for z in range(N_Z) for x in range(N_X)]


def prep_kernel(where, x_ref, cot_ref, own_ref, other_ref, part_ref):
    mine, col = where[0], where[1]
    inputs = x_ref[...]
    gram_act = lax.dot_general(
        inputs, inputs, (((1,), (1,)), ((), ())), preferred_element_type=jnp.float32
    )
    cot = cot_ref[...]
    gram_cot = lax.dot_general(
        cot, cot, (((1,), (1,)), ((), ())), preferred_element_type=jnp.float32
    )
    part_ref[...] = jnp.full(part_ref.shape, jnp.sum(gram_act * gram_cot), jnp.float32)
    for d in range(N_DP):
        for ref, half in ((own_ref, mine), (other_ref, 1 - mine)):
            start = pl.multiple_of(((d * N_MP + half) * N_X + col) * 128, 128)
            ref[d] = x_ref[:, pl.ds(start, 128)].T


def fisher_kernel(n_seq, where, scale, *refs):
    x_refs = refs[:N_X]
    cots = (refs[N_X : N_X + n_seq], refs[N_X + n_seq : N_X + 2 * n_seq])
    w_ref, a_ref, b_ref, lhs = refs[N_X + 2 * n_seq :]
    @pl.when(pl.program_id(0) == 0)
    def _():
        for piece in range(N_X):
            rows = pl.ds(pl.multiple_of(where[piece] * 128, 128), 128)
            for seq in range(n_seq):
                for model in range(2):
                    lhs[model, seq, rows, :] = x_refs[piece][seq, model]

    for block in range(4):
        rows = pl.ds(block * 128, 128)
        weighted = []
        for model in range(2):
            total = jnp.full((128, a_ref.shape[1]), FLOOR, jnp.float32)
            for piece in range(n_seq):
                seq = where[N_X + piece]
                grad = jnp.dot(
                    lhs[model, seq, rows, :],
                    cots[model][piece][...],
                    preferred_element_type=jnp.float32,
                )
                total = total + scale[seq * 2 + model] * (grad * grad)
            weighted.append(total)
        inverse = 1.0 / (weighted[0] + weighted[1])
        a_ref[rows, :] = weighted[0] * inverse * w_ref[rows, :].astype(jnp.float32)
        b_ref[rows, :] = weighted[1] * inverse


def merge_kernel(a_ref, b_ref, w_ref, *refs):
    out_ref = refs[-1]
    out_ref[...] = (a_ref[...] + b_ref[...] * w_ref[...].astype(jnp.float32)).astype(jnp.bfloat16)


def local(activations, gate_pre, hidden_grad, up_weights):
    single = jnp.float32
    width = gate_pre.shape[2]
    m = lax.axis_index("mp").astype(jnp.int32)
    d = lax.axis_index("dp").astype(jnp.int32)
    x = lax.rem(lax.axis_index("tensor").astype(jnp.int32), N_X)
    rows = up_weights.shape[1] // N_MP

    cot = (hidden_grad[0].astype(single) * jax.nn.silu(gate_pre[0].astype(single))).astype(
        jnp.bfloat16
    )
    cot_other = lax.ppermute(cot, "mp", MP_SWAP)

    piece_shape = jax.ShapeDtypeStruct((N_DP, 128, LEN), jnp.bfloat16)
    own_x, other_x, part = pl.pallas_call(
        prep_kernel,
        out_shape=(piece_shape, piece_shape, jax.ShapeDtypeStruct((8, 128), single)),
        grid_spec=pltpu.PrefetchScalarGridSpec(
            num_scalar_prefetch=1,
            grid=(1,),
            in_specs=[
                pl.BlockSpec((LEN, D), lambda i, w: (0, 0)),
                pl.BlockSpec((LEN, width), lambda i, w: (0, 0)),
            ],
            out_specs=[
                pl.BlockSpec((N_DP, 128, LEN), lambda i, w: (0, 0, 0)),
                pl.BlockSpec((N_DP, 128, LEN), lambda i, w: (0, 0, 0)),
                pl.BlockSpec((8, 128), lambda i, w: (0, 0)),
            ],
        ),
        compiler_params=pltpu.CompilerParams(vmem_limit_bytes=VMEM_LIMIT),
        cost_estimate=pl.CostEstimate(flops=4 * 10**8, bytes_accessed=4 * 10**6, transcendentals=0),
        name="prep",
    )(jnp.stack([m, x]), activations[0], cot)

    sent = jnp.broadcast_to(part[None, :1], (N_MP * N_TENSOR, 1, 128))
    parts = exchange(sent, ("mp", "tensor"))
    square = jnp.sum(parts.reshape(N_MP, N_TENSOR, 128), axis=1)
    square = jnp.stack([square[m], square[1 - m]])
    squares = exchange(jnp.broadcast_to(square[None], (N_DP, N_MP, 128)), "dp")
    norm = jnp.sqrt(squares[:, :, 0])
    clip_limit = CLIP_RATIO * math.sqrt(LEN * D * FF)
    factor = clip_limit / jnp.maximum(norm, clip_limit)
    scale = (factor * factor).reshape(-1)

    from_other = lax.ppermute(other_x, "mp", MP_SWAP)
    x_pieces = exchange(jnp.stack([own_x, from_other], axis=1), "dp")
    x_all = [x_pieces] + [lax.ppermute(x_pieces, "tensor", x_shift(k)) for k in (1, -1, 2)]
    x_from = [x, lax.rem(x + 3, 4), lax.rem(x + 1, 4), lax.rem(x + 2, 4)]

    n_chunk = 4
    chunk = rows // n_chunk
    w_mine = up_weights[0]
    w_other = []
    for k in range(n_chunk):
        piece = lax.dynamic_slice(w_mine, ((1 - m) * rows + k * chunk, 0), (chunk, width))
        w_other.append(lax.ppermute(piece, "mp", MP_SWAP))

    y = d // N_CORE
    c = lax.rem(d, N_CORE)
    cots, seqs = [], []
    for value in (cot, cot_other):
        pieces = [value] + [lax.ppermute(value, "dp", y_shift(k)) for k in (1, -1, 2)]
        pieces += [lax.ppermute(piece, "dp", CORE_SWAP) for piece in pieces]
        cots += pieces
    for core in (c, 1 - c):
        for shift in (0, 3, 1, 2):
            seqs.append(lax.rem(y + shift, N_Y) * N_CORE + core)

    tile = 256
    n_seq = N_DP
    where = jnp.stack(x_from + seqs).astype(jnp.int32)
    whole = pl.BlockSpec((N_DP, 2, 128, LEN), lambda i, *_: (0, 0, 0, 0))
    a, b = pl.pallas_call(
        functools.partial(fisher_kernel, n_seq),
        out_shape=(
            jax.ShapeDtypeStruct((rows, width), single),
            jax.ShapeDtypeStruct((rows, width), single),
        ),
        grid_spec=pltpu.PrefetchScalarGridSpec(
            num_scalar_prefetch=2,
            grid=(width // tile,),
            in_specs=[whole] * N_X
            + [pl.BlockSpec((LEN, tile), lambda i, *_: (0, i))] * (2 * n_seq)
            + [pl.BlockSpec((rows, tile), lambda i, w, s: (w[N_X + n_seq], i))],
            out_specs=[pl.BlockSpec((rows, tile), lambda i, *_: (0, i))] * 2,
            scratch_shapes=[pltpu.VMEM((2, n_seq, rows, LEN), jnp.bfloat16)],
        ),
        compiler_params=pltpu.CompilerParams(vmem_limit_bytes=VMEM_LIMIT),
        cost_estimate=pl.CostEstimate(flops=4 * 10**9, bytes_accessed=18 * 10**6, transcendentals=0),
        name="fisher",
    )(jnp.concatenate([where, m[None]]), scale, *x_all, *cots, up_weights[0])

    out = None
    for k in range(n_chunk):
        half = lambda i, k=k: (k, 0)
        first = lambda i: (0, 0)
        in_specs = [pl.BlockSpec((chunk, width), half)] * 2 + [pl.BlockSpec((chunk, width), first)]
        operands = [a, b, w_other[k]]
        aliases = {}
        if out is not None:
            in_specs.append(pl.BlockSpec(memory_space=pl.ANY))
            operands.append(out)
            aliases = {3: 0}
        out = pl.pallas_call(
            merge_kernel,
            out_shape=jax.ShapeDtypeStruct((rows, width), jnp.bfloat16),
            grid=(1,),
            in_specs=in_specs,
            out_specs=pl.BlockSpec((chunk, width), half),
            input_output_aliases=aliases,
            compiler_params=pltpu.CompilerParams(vmem_limit_bytes=VMEM_LIMIT),
            cost_estimate=pl.CostEstimate(
                flops=chunk * width * 2, bytes_accessed=chunk * width * 12, transcendentals=0
            ),
        )(*operands)
    return out


def solution(mesh):
    placed = (
        P("mp", "dp", None),
        P("mp", "dp", "tensor"),
        P("mp", "dp", "tensor"),
        P("mp", "dp", "tensor"),
    )

    return jax.shard_map(
        local, mesh=mesh, in_specs=placed, out_specs=P(("dp", "mp"), "tensor"), check_vma=False
    )
```

time: 318 us -> 190 us (0.60)
  matrix products: 63.9 us -> 0 us
  blocking collectives: 51.7 us -> 0 us
  starting transfers between devices: 24.3 us -> 53.9 us
  Pallas kernels: 0 us -> 23.4 us
  local copies, waits for them, and re-layouts: 31.9 us -> 11.9 us
  other arithmetic: 21.2 us -> 2.39 us
  waiting for transfers between devices: 110 us -> 95.3 us
  between operations: 14.3 us -> 0.19 us
    all_to_all x5 -> x3, waiting for transfers between devices: 110 us -> 20.9 us  [exchange(): return lax.all_to_all(value, axis, 0, 0, tiled=True)]
    ppermute x0 -> x23, waiting for transfers between devices: none -> 74.4 us  [the longest x4 39.1 us: local(): w_other.append(lax.ppermute(piece, 'mp', MP_SWAP))]
    dot_general x10 -> x0, matrix products: 63.9 us -> none  [the longest x8 59.8 us: one_seq(): jnp.einsum('mld,mlf->mdf', acts_models[:, seq_index], cot_piece[:, seq_in...]
    all_to_all x2 -> x0, blocking collectives: 43.3 us -> none  [from_everyone(): lax.all_to_all(jnp.broadcast_to(value[None], (length, *value.shape)), axi...]
    ppermute x0 -> x23, starting transfers between devices: none -> 35.9 us  [the longest x6 13.1 us: local(): lax.ppermute(value, 'dp', y_shift(k))]
    pallas_call x0 -> x6, Pallas kernels: none -> 23.4 us  [the longest x1 13.7 us: local(): pl.pallas_call(functools.partial(fisher_kernel, n_seq), out_shape=(jax.Sh...]
    unnamed x2 -> x0, other arithmetic: 12.7 us -> none
    all_gather x1 -> x0, blocking collectives: 8.41 us -> none  [local(): lax.all_gather(for_sending(both_clip), 'dp', axis=1, tiled=True)]
  transfers between devices with their start and end apart: 6 -> 26, of which waited for: 3 -> 11; matrix products, arithmetic and copies ran while one was open for 34% -> 3% of each run, Pallas kernels for 0% -> 11%
where the time goes in v1:
time: 190 us; the launch traced here: 187 us
  waiting for transfers between devices  95.3 us (50%)
  starting transfers between devices  53.9 us (28%)
  Pallas kernels  23.4 us (12%)
  local copies, waits for them, and re-layouts  11.9 us (6%)
  other arithmetic  2.39 us (1%)
    ppermute x4, waiting for transfers between devices, local(): w_other.append(lax.ppermute(piece, 'mp', MP_SWAP))  39.1 us
    ppermute x1, waiting for transfers between devices, local(): from_other = lax.ppermute(other_x, 'mp', MP_SWAP)  21.9 us
    all_to_all x3, waiting for transfers between devices, exchange(): return lax.all_to_all(value, axis, 0, 0, tiled=True)  20.9 us
    all_to_all x3, starting transfers between devices, exchange(): return lax.all_to_all(value, axis, 0, 0, tiled=True)  18 us
    pallas_call x1, Pallas kernels, local(): pl.pallas_call(functools.partial(fisher_kernel, n_seq), out_shape=(jax.Sh...  13.7 us
    ppermute x6, starting transfers between devices, local(): lax.ppermute(value, 'dp', y_shift(k))  13.1 us
    ppermute x4, starting transfers between devices, local(): w_other.append(lax.ppermute(piece, 'mp', MP_SWAP))  11.9 us
    ppermute x3, waiting for transfers between devices, local(): lax.ppermute(x_pieces, 'tensor', x_shift(k))  8.47 us
  transfers between devices with their start and end apart: 26, of which 11 were waited for; matrix products, arithmetic and copies ran while one was open for 3% of the time, Pallas kernels for 11%

profile of v1, /device:TPU:38, one launch (start us, length us, event | category | flops | bytes accessed | tf_op | source)
XLA Modules:
  0.0 187.2 jit_solution(13434002132883182206)
XLA Ops:
  1.4 6.4 %collective-permute-start.11 = (bf16[128,1792]{1,0:T(8,128)(2,1)S(1)}, bf16[128,1792]{1,0:T(8,128)(2,1)}, u32[]{:S(2)}, u32[]{:S(2)}) collective-permute-start(bf16[128,1792]{1,0:T(8,128)(2,1)S(1)} %fusion.4.cot_ref.refs_4_), channel_id=1, source_target_pairs={{0,128},{128,0},{1,129},{129,1},{2,130},{130,2},{3,131},{131,3},{4... | collective-permute-start | bytes 1376264 | tf_op jit(solution)/shard_map/ppermute | solution.py:105
  7.8 3.2 %collective-permute-start.6 = (bf16[128,1792]{1,0:T(8,128)(2,1)S(1)}, bf16[128,1792]{1,0:T(8,128)(2,1)S(1)}, u32[]{:S(2)}, u32[]{:S(2)}) collective-permute-start(bf16[128,1792]{1,0:T(8,128)(2,1)S(1)} %fusion.4.cot_ref.refs_4_), channel_id=1, source_target_pairs={{0,64},{16,80},{32,96},{48,112},{64,0},{80,16},{96,32},{112,48},{1... | collective-permute-start | bytes 1376264 | tf_op jit(solution)/shard_map/ppermute | solution.py:156
  15.1 2.6 %collective-permute-start.5 = (bf16[128,1792]{1,0:T(8,128)(2,1)S(1)}, bf16[128,1792]{1,0:T(8,128)(2,1)S(1)}, u32[]{:S(2)}, u32[]{:S(2)}) collective-permute-start(bf16[128,1792]{1,0:T(8,128)(2,1)S(1)} %fusion.4.cot_ref.refs_4_), channel_id=1, source_target_pairs={{0,96},{16,112},{32,0},{48,16},{64,32},{80,48},{96,64},{112,80},{1... | collective-permute-start | bytes 1376264 | tf_op jit(solution)/shard_map/ppermute | solution.py:156
  17.6 21.9 %collective-permute-done = bf16[8,128,128]{2,1,0:T(8,128)(2,1)S(1)} collective-permute-done((bf16[8,128,128]{2,1,0:T(8,128)(2,1)S(1)}, bf16[8,128,128]{2,1,0:T(8,128)(2,1)S(1)}, u32[]{:S(2)}, u32[]{:S(2)}) %collective-permute-start) | collective-permute-done | bytes 262176 | tf_op jit(solution)/shard_map/ppermute | solution.py:139
  43.6 4.2 %all-to-all-start.2 = ((bf16[8,2,128,128]{3,2,1,0:T(8,128)(2,1)}), bf16[8,2,128,128]{3,2,1,0:T(8,128)(2,1)}, u32[]{:S(2)}, u32[]{:S(2)}) async-start(bf16[8,2,128,128]{3,2,1,0:T(8,128)(2,1)} %pad_maximum_fusion), calls=%async_computation.2 | async-start | bytes 1048576 | tf_op jit(solution)/shard_map/all_to_all | solution.py:28
  47.7 3.4 %collective-permute-start.14 = (bf16[128,1792]{1,0:T(8,128)(2,1)}, bf16[128,1792]{1,0:T(8,128)(2,1)}, u32[]{:S(2)}, u32[]{:S(2)}) collective-permute-start(bf16[128,1792]{1,0:T(8,128)(2,1)} %collective-permute-done.11.refs_12_), channel_id=1, source_target_pairs={{0,64},{16,80},{32,96},{48,112},{64,0},{80,16},{96,32},{112,48},{1... | collective-permute-start | bytes 1376264 | tf_op jit(solution)/shard_map/ppermute | solution.py:156
  51.7 2.7 %collective-permute-done.12.refs_13_ = bf16[128,1792]{1,0:T(8,128)(2,1)} collective-permute-done((bf16[128,1792]{1,0:T(8,128)(2,1)}, bf16[128,1792]{1,0:T(8,128)(2,1)}, u32[]{:S(2)}, u32[]{:S(2)}) %collective-permute-start.12) | collective-permute-done | bytes 458784 | tf_op jit(solution)/shard_map/ppermute | solution.py:156
  54.9 13.9 %all-to-all-done.2.refs_0_ = bf16[8,2,128,128]{3,2,1,0:T(8,128)(2,1)} async-done(((bf16[8,2,128,128]{3,2,1,0:T(8,128)(2,1)}), bf16[8,2,128,128]{3,2,1,0:T(8,128)(2,1)}, u32[]{:S(2)}, u32[]{:S(2)}) %all-to-all-start.2) | async-done | bytes 524320 | tf_op jit(solution)/shard_map/all_to_all | solution.py:28
  71.7 10.6 %all-to-all-start = ((f32[32,1,128]{2,1,0:T(1,128)}), f32[32,1,128]{2,1,0:T(1,128)S(1)}, u32[]{:S(2)}, u32[]{:S(2)}) async-start(f32[32,1,128]{2,1,0:T(1,128)} %broadcast_in_dim.19), calls=%async_computation | async-start | bytes 32768 | tf_op jit(solution)/shard_map/all_to_all | solution.py:28
  84.4 4.9 %all-to-all-done = f32[32,1,128]{2,1,0:T(1,128)S(1)} async-done(((f32[32,1,128]{2,1,0:T(1,128)}), f32[32,1,128]{2,1,0:T(1,128)S(1)}, u32[]{:S(2)}, u32[]{:S(2)}) %all-to-all-start) | async-done | bytes 16416 | tf_op jit(solution)/shard_map/all_to_all | solution.py:28
  90.8 3.3 %all-to-all-start.1 = ((f32[8,2,128]{2,1,0:T(2,128)}), f32[8,2,128]{2,1,0:T(2,128)S(1)}, u32[]{:S(2)}, u32[]{:S(2)}) async-start(f32[8,2,128]{2,1,0:T(2,128)} %broadcast_in_dim.20), calls=%async_computation.1 | async-start | bytes 16384 | tf_op jit(solution)/shard_map/all_to_all | solution.py:28
  94.5 2.7 %dynamic-slice_bitcast_fusion = (bf16[128,1792]{1,0:T(8,128)(2,1)}, bf16[128,1792]{1,0:T(8,128)(2,1)}, bf16[128,1792]{1,0:T(8,128)(2,1)}, bf16[128,1792]{1,0:T(8,128)(2,1)}) fusion(bf16[1,1024,1792]{2,1,0:T(8,128)(2,1)} %param.7, s32[]{:T(128)S(6)} %select_n.29, s32[]{:T(128)S(6)} %select_n.27, s32[]{:T(128)S(6)} %select_n.26, s32[]{:T(128)S(6)} %select_n.28), kind=kLoop, calls=%fused_computation.8 | loop fusion | bytes 3670032 | tf_op jit(solution)/shard_map/dynamic_slice | solution.py:149
  97.3 2.1 %all-to-all-done.1 = f32[8,2,128]{2,1,0:T(2,128)S(1)} async-done(((f32[8,2,128]{2,1,0:T(2,128)}), f32[8,2,128]{2,1,0:T(2,128)S(1)}, u32[]{:S(2)}, u32[]{:S(2)}) %all-to-all-start.1) | async-done | bytes 8224 | tf_op jit(solution)/shard_map/all_to_all | solution.py:28
  99.4 8.5 %collective-permute-done.2.refs_2_ = bf16[8,2,128,128]{3,2,1,0:T(8,128)(2,1)} collective-permute-done((bf16[8,2,128,128]{3,2,1,0:T(8,128)(2,1)}, bf16[8,2,128,128]{3,2,1,0:T(8,128)(2,1)}, u32[]{:S(2)}, u32[]{:S(2)}) %collective-permute-start.2) | collective-permute-done | bytes 524320 | tf_op jit(solution)/shard_map/ppermute | solution.py:141
  107.9 4.5 %collective-permute-start.22 = (bf16[128,1792]{1,0:T(8,128)(2,1)}, bf16[128,1792]{1,0:T(8,128)(2,1)S(1)}, u32[]{:S(2)}, u32[]{:S(2)}) collective-permute-start(bf16[128,1792]{1,0:T(8,128)(2,1)} %get-tuple-element.15), channel_id=1, source_target_pairs={{0,128},{128,0},{1,129},{129,1},{2,130},{130,2},{3,131},{131,3},{4... | collective-permute-start | bytes 1376264 | tf_op jit(solution)/shard_map/ppermute | solution.py:150
  113.9 4.5 %collective-permute-start.20 = (bf16[128,1792]{1,0:T(8,128)(2,1)}, bf16[128,1792]{1,0:T(8,128)(2,1)S(1)}, u32[]{:S(2)}, u32[]{:S(2)}) collective-permute-start(bf16[128,1792]{1,0:T(8,128)(2,1)} %get-tuple-element.16), channel_id=1, source_target_pairs={{0,128},{128,0},{1,129},{129,1},{2,130},{130,2},{3,131},{131,3},{4... | collective-permute-start | bytes 1376264 | tf_op jit(solution)/shard_map/ppermute | solution.py:150
  124.1 13.7 %fisher.1 = (f32[512,1792]{1,0:T(8,128)}, f32[512,1792]{1,0:T(8,128)}) custom-call(s32[13]{0:T(128)S(1)} %concatenate.3.where, f32[16]{0:T(128)S(1)} %mul.43.scale, bf16[8,2,128,128]{3,2,1,0:T(8,128)(2,1)} %all-to-all-done.2.refs_0_, bf16[8,2,128,128]{3,2,1,0:T(8,128)(2,1)} %collective-permute-done.1.refs_1_, ...), custom_call_target="tpu_custom_call" | custom-call | flops 4000000000 | bytes 18000000 | tf_op jit(solution)/shard_map/fisher/pallas_call | solution.py:167
  139.8 2.1 %shard_map.46.refs_0_ = bf16[512,1792]{1,0:T(8,128)(2,1)} custom-call(f32[512,1792]{1,0:T(8,128)S(1)} %copy-done, f32[512,1792]{1,0:T(8,128)} %get-tuple-element.14.b_ref, bf16[128,1792]{1,0:T(8,128)(2,1)S(1)} %collective-permute-done.22.w_ref), custom_call_target="tpu_custom_call" | custom-call | flops 458752 | bytes 2752512 | tf_op jit(solution)/shard_map/pallas_call | solution.py:198
  141.9 16.2 %collective-permute-done.21.w_ref = bf16[128,1792]{1,0:T(8,128)(2,1)S(1)} collective-permute-done((bf16[128,1792]{1,0:T(8,128)(2,1)}, bf16[128,1792]{1,0:T(8,128)(2,1)S(1)}, u32[]{:S(2)}, u32[]{:S(2)}) %collective-permute-start.21) | collective-permute-done | bytes 458784 | tf_op jit(solution)/shard_map/ppermute | solution.py:150
  158.1 2.1 %shard_map.47.refs_0_ = bf16[512,1792]{1,0:T(8,128)(2,1)} custom-call(f32[512,1792]{1,0:T(8,128)S(1)} %copy-done, f32[512,1792]{1,0:T(8,128)} %get-tuple-element.14.b_ref, bf16[128,1792]{1,0:T(8,128)(2,1)S(1)} %collective-permute-done.21.w_ref, bf16[512,1792]{1,0:T(8,128)(2,1)} %shard_map.46.refs_0_), custom_call_target="tpu_custom_call", output_to_operand_aliasing={{}: (3, {})} | custom-call | flops 458752 | bytes 2752512 | tf_op jit(solution)/shard_map/pallas_call | solution.py:198
  160.1 19.8 %collective-permute-done.20.w_ref = bf16[128,1792]{1,0:T(8,128)(2,1)S(1)} collective-permute-done((bf16[128,1792]{1,0:T(8,128)(2,1)}, bf16[128,1792]{1,0:T(8,128)(2,1)S(1)}, u32[]{:S(2)}, u32[]{:S(2)}) %collective-permute-start.20) | collective-permute-done | bytes 458784 | tf_op jit(solution)/shard_map/ppermute | solution.py:150
  179.9 2.1 %shard_map.48.refs_0_ = bf16[512,1792]{1,0:T(8,128)(2,1)} custom-call(f32[512,1792]{1,0:T(8,128)S(1)} %copy-done, f32[512,1792]{1,0:T(8,128)} %get-tuple-element.14.b_ref, bf16[128,1792]{1,0:T(8,128)(2,1)S(1)} %collective-permute-done.20.w_ref, bf16[512,1792]{1,0:T(8,128)(2,1)} %shard_map.47.refs_0_), custom_call_target="tpu_custom_call", output_to_operand_aliasing={{}: (3, {})} | custom-call | flops 458752 | bytes 2752512 | tf_op jit(solution)/shard_map/pallas_call | solution.py:198
  182.0 3.1 %collective-permute-done.19.w_ref = bf16[128,1792]{1,0:T(8,128)(2,1)S(1)} collective-permute-done((bf16[128,1792]{1,0:T(8,128)(2,1)}, bf16[128,1792]{1,0:T(8,128)(2,1)S(1)}, u32[]{:S(2)}, u32[]{:S(2)}) %collective-permute-start.19) | collective-permute-done | bytes 458784 | tf_op jit(solution)/shard_map/ppermute | solution.py:150
  185.1 2.1 %shard_map.49 = bf16[512,1792]{1,0:T(8,128)(2,1)} custom-call(f32[512,1792]{1,0:T(8,128)S(1)} %copy-done, f32[512,1792]{1,0:T(8,128)} %get-tuple-element.14.b_ref, bf16[128,1792]{1,0:T(8,128)(2,1)S(1)} %collective-permute-done.19.w_ref, bf16[512,1792]{1,0:T(8,128)(2,1)} %shard_map.48.refs_0_), custom_call_target="tpu_custom_call", output_to_operand_aliasing={{}: (3, {})} | custom-call | flops 458752 | bytes 2752512 | tf_op jit(solution)/shard_map/pallas_call | solution.py:198
  (69 shorter events, 26.8 us)
Async XLA Ops:
  1.4 38.0 %collective-permute-start.11 = (bf16[128,1792]{1,0:T(8,128)(2,1)S(1)}, bf16[128,1792]{1,0:T(8,128)(2,1)}, u32[]{:S(2)}, u32[]{:S(2)}) collective-permute-start(bf16[128,1792]{1,0:T(8,128)(2,1)S(1)} %fusion.4.cot_ref.refs_4_), channel_id=1, source_target_pairs={{0,128},{128,0},{1,129},{129,1},{2,130},{130,2},{3,131},{131,3},{4... | collective-permute-start | bytes 1376264 | tf_op jit(solution)/shard_map/ppermute | solution.py:105
  7.8 33.2 %collective-permute-start.6 = (bf16[128,1792]{1,0:T(8,128)(2,1)S(1)}, bf16[128,1792]{1,0:T(8,128)(2,1)S(1)}, u32[]{:S(2)}, u32[]{:S(2)}) collective-permute-start(bf16[128,1792]{1,0:T(8,128)(2,1)S(1)} %fusion.4.cot_ref.refs_4_), channel_id=1, source_target_pairs={{0,64},{16,80},{32,96},{48,112},{64,0},{80,16},{96,32},{112,48},{1... | collective-permute-start | bytes 1376264 | tf_op jit(solution)/shard_map/ppermute | solution.py:156
  14.2 25.3 %collective-permute-start = (bf16[8,128,128]{2,1,0:T(8,128)(2,1)S(1)}, bf16[8,128,128]{2,1,0:T(8,128)(2,1)S(1)}, u32[]{:S(2)}, u32[]{:S(2)}) collective-permute-start(bf16[8,128,128]{2,1,0:T(8,128)(2,1)S(1)} %get-tuple-element.12), channel_id=1, source_target_pairs={{0,128},{128,0},{1,129},{129,1},{2,130},{130,2},{3,131},{131,3},{4... | collective-permute-start | bytes 786440 | tf_op jit(solution)/shard_map/ppermute | solution.py:139
  14.4 33.3 %collective-permute-start.4 = (bf16[128,1792]{1,0:T(8,128)(2,1)S(1)}, bf16[128,1792]{1,0:T(8,128)(2,1)S(1)}, u32[]{:S(2)}, u32[]{:S(2)}) collective-permute-start(bf16[128,1792]{1,0:T(8,128)(2,1)S(1)} %fusion.4.cot_ref.refs_4_), channel_id=1, source_target_pairs={{0,32},{16,48},{32,64},{48,80},{64,96},{80,112},{96,0},{112,16},{1... | collective-permute-start | bytes 1376264 | tf_op jit(solution)/shard_map/ppermute | solution.py:156
  15.1 36.1 %collective-permute-start.5 = (bf16[128,1792]{1,0:T(8,128)(2,1)S(1)}, bf16[128,1792]{1,0:T(8,128)(2,1)S(1)}, u32[]{:S(2)}, u32[]{:S(2)}) collective-permute-start(bf16[128,1792]{1,0:T(8,128)(2,1)S(1)} %fusion.4.cot_ref.refs_4_), channel_id=1, source_target_pairs={{0,96},{16,112},{32,0},{48,16},{64,32},{80,48},{96,64},{112,80},{1... | collective-permute-start | bytes 1376264 | tf_op jit(solution)/shard_map/ppermute | solution.py:156
  39.5 14.9 %collective-permute-start.12 = (bf16[128,1792]{1,0:T(8,128)(2,1)}, bf16[128,1792]{1,0:T(8,128)(2,1)}, u32[]{:S(2)}, u32[]{:S(2)}) collective-permute-start(bf16[128,1792]{1,0:T(8,128)(2,1)} %collective-permute-done.11.refs_12_), channel_id=1, source_target_pairs={{0,32},{16,48},{32,64},{48,80},{64,96},{80,112},{96,0},{112,16},{1... | collective-permute-start | bytes 1376264 | tf_op jit(solution)/shard_map/ppermute | solution.py:156
  41.1 13.7 %collective-permute-start.13 = (bf16[128,1792]{1,0:T(8,128)(2,1)}, bf16[128,1792]{1,0:T(8,128)(2,1)}, u32[]{:S(2)}, u32[]{:S(2)}) collective-permute-start(bf16[128,1792]{1,0:T(8,128)(2,1)} %collective-permute-done.11.refs_12_), channel_id=1, source_target_pairs={{0,96},{16,112},{32,0},{48,16},{64,32},{80,48},{96,64},{112,80},{1... | collective-permute-start | bytes 1376264 | tf_op jit(solution)/shard_map/ppermute | solution.py:156
  43.6 25.3 %all-to-all-start.2 = ((bf16[8,2,128,128]{3,2,1,0:T(8,128)(2,1)}), bf16[8,2,128,128]{3,2,1,0:T(8,128)(2,1)}, u32[]{:S(2)}, u32[]{:S(2)}) async-start(bf16[8,2,128,128]{3,2,1,0:T(8,128)(2,1)} %pad_maximum_fusion), calls=%async_computation.2 | async-start | bytes 1048576 | tf_op jit(solution)/shard_map/all_to_all | solution.py:28
  47.7 22.9 %collective-permute-start.14 = (bf16[128,1792]{1,0:T(8,128)(2,1)}, bf16[128,1792]{1,0:T(8,128)(2,1)}, u32[]{:S(2)}, u32[]{:S(2)}) collective-permute-start(bf16[128,1792]{1,0:T(8,128)(2,1)} %collective-permute-done.11.refs_12_), channel_id=1, source_target_pairs={{0,64},{16,80},{32,96},{48,112},{64,0},{80,16},{96,32},{112,48},{1... | collective-permute-start | bytes 1376264 | tf_op jit(solution)/shard_map/ppermute | solution.py:156
  51.1 31.2 %collective-permute-start.15 = (bf16[128,1792]{1,0:T(8,128)(2,1)}, bf16[128,1792]{1,0:T(8,128)(2,1)}, u32[]{:S(2)}, u32[]{:S(2)}) collective-permute-start(bf16[128,1792]{1,0:T(8,128)(2,1)} %collective-permute-done.11.refs_12_), channel_id=1, source_target_pairs={{0,16},{16,0},{32,48},{48,32},{64,80},{80,64},{96,112},{112,96},{1... | collective-permute-start | bytes 1376264 | tf_op jit(solution)/shard_map/ppermute | solution.py:157
  51.2 32.1 %collective-permute-start.10 = (bf16[128,1792]{1,0:T(8,128)(2,1)S(1)}, bf16[128,1792]{1,0:T(8,128)(2,1)S(1)}, u32[]{:S(2)}, u32[]{:S(2)}) collective-permute-start(bf16[128,1792]{1,0:T(8,128)(2,1)S(1)} %collective-permute-done.6.refs_7_), channel_id=1, source_target_pairs={{0,16},{16,0},{32,48},{48,32},{64,80},{80,64},{96,112},{112,96},{1... | collective-permute-start | bytes 1376264 | tf_op jit(solution)/shard_map/ppermute | solution.py:157
  54.4 35.0 %collective-permute-start.8 = (bf16[128,1792]{1,0:T(8,128)(2,1)S(1)}, bf16[128,1792]{1,0:T(8,128)(2,1)S(1)}, u32[]{:S(2)}, u32[]{:S(2)}) collective-permute-start(bf16[128,1792]{1,0:T(8,128)(2,1)S(1)} %collective-permute-done.4.refs_5_), channel_id=1, source_target_pairs={{0,16},{16,0},{32,48},{48,32},{64,80},{80,64},{96,112},{112,96},{1... | collective-permute-start | bytes 1376264 | tf_op jit(solution)/shard_map/ppermute | solution.py:157
  54.8 34.9 %collective-permute-start.9 = (bf16[128,1792]{1,0:T(8,128)(2,1)S(1)}, bf16[128,1792]{1,0:T(8,128)(2,1)}, u32[]{:S(2)}, u32[]{:S(2)}) collective-permute-start(bf16[128,1792]{1,0:T(8,128)(2,1)S(1)} %collective-permute-done.5.refs_6_), channel_id=1, source_target_pairs={{0,16},{16,0},{32,48},{48,32},{64,80},{80,64},{96,112},{112,96},{1... | collective-permute-start | bytes 1376264 | tf_op jit(solution)/shard_map/ppermute | solution.py:157
  70.6 23.5 %collective-permute-start.1 = (bf16[8,2,128,128]{3,2,1,0:T(8,128)(2,1)}, bf16[8,2,128,128]{3,2,1,0:T(8,128)(2,1)}, u32[]{:S(2)}, u32[]{:S(2)}) collective-permute-start(bf16[8,2,128,128]{3,2,1,0:T(8,128)(2,1)} %all-to-all-done.2.refs_0_), channel_id=1, source_target_pairs={{0,1},{1,2},{2,3},{3,0},{4,5},{5,6},{6,7},{7,4},{8,9},{9,10},{10,1... | collective-permute-start | bytes 1572872 | tf_op jit(solution)/shard_map/ppermute | solution.py:141
  71.7 17.6 %all-to-all-start = ((f32[32,1,128]{2,1,0:T(1,128)}), f32[32,1,128]{2,1,0:T(1,128)S(1)}, u32[]{:S(2)}, u32[]{:S(2)}) async-start(f32[32,1,128]{2,1,0:T(1,128)} %broadcast_in_dim.19), calls=%async_computation | async-start | bytes 32768 | tf_op jit(solution)/shard_map/all_to_all | solution.py:28
  82.3 25.6 %collective-permute-start.2 = (bf16[8,2,128,128]{3,2,1,0:T(8,128)(2,1)}, bf16[8,2,128,128]{3,2,1,0:T(8,128)(2,1)}, u32[]{:S(2)}, u32[]{:S(2)}) collective-permute-start(bf16[8,2,128,128]{3,2,1,0:T(8,128)(2,1)} %all-to-all-done.2.refs_0_), channel_id=1, source_target_pairs={{0,3},{1,0},{2,1},{3,2},{4,7},{5,4},{6,5},{7,6},{8,11},{9,8},{10,9... | collective-permute-start | bytes 1572872 | tf_op jit(solution)/shard_map/ppermute | solution.py:141
  83.3 29.1 %collective-permute-start.3 = (bf16[8,2,128,128]{3,2,1,0:T(8,128)(2,1)}, bf16[8,2,128,128]{3,2,1,0:T(8,128)(2,1)}, u32[]{:S(2)}, u32[]{:S(2)}) collective-permute-start(bf16[8,2,128,128]{3,2,1,0:T(8,128)(2,1)} %all-to-all-done.2.refs_0_), channel_id=1, source_target_pairs={{0,2},{1,3},{2,0},{3,1},{4,6},{5,7},{6,4},{7,5},{8,10},{9,11},{10,... | collective-permute-start | bytes 1572872 | tf_op jit(solution)/shard_map/ppermute | solution.py:141
  89.4 24.5 %collective-permute-start.16 = (bf16[128,1792]{1,0:T(8,128)(2,1)}, bf16[128,1792]{1,0:T(8,128)(2,1)}, u32[]{:S(2)}, u32[]{:S(2)}) collective-permute-start(bf16[128,1792]{1,0:T(8,128)(2,1)} %collective-permute-done.12.refs_13_), channel_id=1, source_target_pairs={{0,16},{16,0},{32,48},{48,32},{64,80},{80,64},{96,112},{112,96},{1... | collective-permute-start | bytes 1376264 | tf_op jit(solution)/shard_map/ppermute | solution.py:157
  89.7 28.6 %collective-permute-start.17 = (bf16[128,1792]{1,0:T(8,128)(2,1)}, bf16[128,1792]{1,0:T(8,128)(2,1)}, u32[]{:S(2)}, u32[]{:S(2)}) collective-permute-start(bf16[128,1792]{1,0:T(8,128)(2,1)} %collective-permute-done.13.refs_14_), channel_id=1, source_target_pairs={{0,16},{16,0},{32,48},{48,32},{64,80},{80,64},{96,112},{112,96},{1... | collective-permute-start | bytes 1376264 | tf_op jit(solution)/shard_map/ppermute | solution.py:157
  94.1 25.9 %collective-permute-start.18 = (bf16[128,1792]{1,0:T(8,128)(2,1)}, bf16[128,1792]{1,0:T(8,128)(2,1)}, u32[]{:S(2)}, u32[]{:S(2)}) collective-permute-start(bf16[128,1792]{1,0:T(8,128)(2,1)} %collective-permute-done.14.refs_15_), channel_id=1, source_target_pairs={{0,16},{16,0},{32,48},{48,32},{64,80},{80,64},{96,112},{112,96},{1... | collective-permute-start | bytes 1376264 | tf_op jit(solution)/shard_map/ppermute | solution.py:157
  107.9 29.9 %collective-permute-start.22 = (bf16[128,1792]{1,0:T(8,128)(2,1)}, bf16[128,1792]{1,0:T(8,128)(2,1)S(1)}, u32[]{:S(2)}, u32[]{:S(2)}) collective-permute-start(bf16[128,1792]{1,0:T(8,128)(2,1)} %get-tuple-element.15), channel_id=1, source_target_pairs={{0,128},{128,0},{1,129},{129,1},{2,130},{130,2},{3,131},{131,3},{4... | collective-permute-start | bytes 1376264 | tf_op jit(solution)/shard_map/ppermute | solution.py:150
  112.4 45.7 %collective-permute-start.21 = (bf16[128,1792]{1,0:T(8,128)(2,1)}, bf16[128,1792]{1,0:T(8,128)(2,1)S(1)}, u32[]{:S(2)}, u32[]{:S(2)}) collective-permute-start(bf16[128,1792]{1,0:T(8,128)(2,1)} %get-tuple-element.18), channel_id=1, source_target_pairs={{0,128},{128,0},{1,129},{129,1},{2,130},{130,2},{3,131},{131,3},{4... | collective-permute-start | bytes 1376264 | tf_op jit(solution)/shard_map/ppermute | solution.py:150
  113.9 66.0 %collective-permute-start.20 = (bf16[128,1792]{1,0:T(8,128)(2,1)}, bf16[128,1792]{1,0:T(8,128)(2,1)S(1)}, u32[]{:S(2)}, u32[]{:S(2)}) collective-permute-start(bf16[128,1792]{1,0:T(8,128)(2,1)} %get-tuple-element.16), channel_id=1, source_target_pairs={{0,128},{128,0},{1,129},{129,1},{2,130},{130,2},{3,131},{131,3},{4... | collective-permute-start | bytes 1376264 | tf_op jit(solution)/shard_map/ppermute | solution.py:150
  118.3 66.8 %collective-permute-start.19 = (bf16[128,1792]{1,0:T(8,128)(2,1)}, bf16[128,1792]{1,0:T(8,128)(2,1)S(1)}, u32[]{:S(2)}, u32[]{:S(2)}) collective-permute-start(bf16[128,1792]{1,0:T(8,128)(2,1)} %get-tuple-element.17), channel_id=1, source_target_pairs={{0,128},{128,0},{1,129},{129,1},{2,130},{130,2},{3,131},{131,3},{4... | collective-permute-start | bytes 1376264 | tf_op jit(solution)/shard_map/ppermute | solution.py:150
  (12 other events, 205.5 us)

commit v2 on v1

v2 whole, which is shorter than its diff:
```python
import functools
import math

import jax
import jax.numpy as jnp
from jax import lax
from jax.experimental import pallas as pl
from jax.experimental.pallas import tpu as pltpu
from jax.sharding import PartitionSpec as P


D = 8192
FF = 28672
LEN = 128
CLIP_RATIO = 0.05
FLOOR = 0.1

N_Y, N_CORE, N_Z, N_X = 4, 2, 4, 4
N_DP = N_Y * N_CORE
N_MP = 2
MP_SWAP = [(0, 1), (1, 0)]
Z_SWAP = [(z * N_X + x, (z ^ 1) * N_X + x) for z in range(N_Z) for x in range(N_X)]
HALF = N_DP // 2
CORE_SWAP = [(i, i ^ 1) for i in range(N_DP)]
VMEM_LIMIT = 50 * 1024 * 1024
PREP_VMEM_LIMIT = 63 * 1024 * 1024


CHUNKS = ((384, 128), (0, 256), (288, 96), (256, 32))
Z_GROUPS = [
    [(m * N_Z + z) * N_X + x for m in range(N_MP) for z in range(N_Z)] for x in range(N_X)
]
N_Z_ALL = N_MP * N_Z
TAIL = 8


def exchange(value, axis, groups=None):
    return lax.all_to_all(value, axis, 0, 0, axis_index_groups=groups, tiled=True)


def y_shift(k):
    return [
        (y * N_CORE + c, (y + k) % N_Y * N_CORE + c) for y in range(N_Y) for c in range(N_CORE)
    ]


def x_shift(k):
    return [(z * N_X + x, z * N_X + (x + k) % N_X) for z in range(N_Z) for x in range(N_X)]


def piece_kernel(where, *refs):
    *x_refs, w_ref, out_ref, chunk_ref = refs
    for d, ref in enumerate(x_refs):
        out_ref[d] = ref[...].T
    chunk_ref[...] = w_ref[...]


def prep_kernel(where, x_hbm, gate_ref, grad_ref, own_ref, cot_ref, part_ref, x_ref, arrived):
    mine, col = where[0], where[1]
    parts = x_ref.shape[0]
    copies = [
        pltpu.make_async_copy(
            x_hbm.at[:, pl.ds(k * x_ref.shape[2], x_ref.shape[2])], x_ref.at[k], arrived.at[k]
        )
        for k in range(parts)
    ]
    for copy in copies:
        copy.start()
    gate = gate_ref[...].astype(jnp.float32)
    silu = gate / (1.0 + jnp.exp(-gate))
    cot = (grad_ref[...].astype(jnp.float32) * silu).astype(jnp.bfloat16)
    cot_ref[...] = cot
    gram_cot = lax.dot_general(
        cot, cot, (((1,), (1,)), ((), ())), preferred_element_type=jnp.float32
    )
    gram_act = jnp.zeros((LEN, LEN), jnp.float32)
    share = N_DP // parts
    for k in range(parts):
        copies[k].wait()
        inputs = x_ref[k]
        gram_act += lax.dot_general(
            inputs, inputs, (((1,), (1,)), ((), ())), preferred_element_type=jnp.float32
        )
        for d in range(share):
            start = pl.multiple_of(((d * N_MP + mine) * N_X + col) * 128, 128)
            own_ref[k * share + d] = x_ref[k, :, pl.ds(start, 128)].T
    part_ref[...] = jnp.full(part_ref.shape, jnp.sum(gram_act * gram_cot), jnp.float32)


def pack_kernel(where, own_ref, kept_ref, swapped_ref, part_ref, out_ref):
    parity = where[2]
    rows = []
    for model in range(N_MP):
        rest = jnp.sum(part_ref[pl.ds(model * N_Z, N_Z), 0, :], axis=0, keepdims=True)
        for _ in range(3):
            short = rest.astype(jnp.bfloat16).astype(jnp.float32)
            rows.append(short)
            rest = rest - short
    rows.append(jnp.zeros((TAIL - len(rows), 128), jnp.float32))
    tail = jnp.concatenate(rows, axis=0).astype(jnp.bfloat16)
    for d in range(N_DP):
        out_ref[d, 0, pl.ds(0, 128), :] = own_ref[d]
        for model in range(2):
            out_ref[d, model, pl.ds(128, TAIL), :] = tail
    for half, ref in ((parity, kept_ref), (1 - parity, swapped_ref)):
        for d in range(HALF):
            out_ref[half * HALF + d, 1, pl.ds(0, 128), :] = ref[d]


def fisher_kernel(n_seq, where, *refs):
    x_refs = refs[:N_X]
    cots = (refs[N_X : N_X + n_seq], refs[N_X + n_seq : N_X + 2 * n_seq])
    w_ref, a_ref, b_ref, lhs, scale = refs[N_X + 2 * n_seq :]
    first = where[N_X + n_seq] == 0
    limit = CLIP_RATIO * math.sqrt(LEN * D * FF)

    @pl.when(pl.program_id(0) == 0)
    def _():
        for piece in range(N_X):
            rows = pl.ds(pl.multiple_of(where[piece] * 128, 128), 128)
            for seq in range(n_seq):
                for model in range(2):
                    lhs[model, seq, rows, :] = x_refs[piece][seq, model, pl.ds(0, 128), :]
        for seq in range(n_seq):
            tails = sum(
                ref[seq, 0, pl.ds(128, TAIL), :].astype(jnp.float32) for ref in x_refs
            )
            squares = [tails[3 * k : 3 * k + 1] + tails[3 * k + 1 : 3 * k + 2] + tails[3 * k + 2 : 3 * k + 3] for k in range(2)]
            for model in range(2):
                square = jnp.where(first, squares[model], squares[1 - model])
                factor = limit / jnp.maximum(jnp.sqrt(square), limit)
                clip = factor * factor
                scale[model, seq] = jnp.broadcast_to(
                    jnp.concatenate([clip] * (scale.shape[3] // 128), axis=1), scale.shape[2:]
                )

    for block in range(4):
        rows = pl.ds(block * 128, 128)
        weighted = []
        for model in range(2):
            total = jnp.full((128, a_ref.shape[1]), FLOOR, jnp.float32)
            for piece in range(n_seq):
                seq = where[N_X + piece]
                grad = jnp.dot(
                    lhs[model, seq, rows, :],
                    cots[model][piece][...],
                    preferred_element_type=jnp.float32,
                )
                total = total + scale[model, seq, pl.ds(0, 1), :] * (grad * grad)
            weighted.append(total)
        inverse = 1.0 / (weighted[0] + weighted[1])
        a_ref[rows, :] = weighted[0] * inverse * w_ref[rows, :].astype(jnp.float32)
        b_ref[rows, :] = weighted[1] * inverse


def merge_kernel(a_ref, b_ref, w_ref, *refs):
    out_ref = refs[-1]
    out_ref[...] = (a_ref[...] + b_ref[...] * w_ref[...].astype(jnp.float32)).astype(jnp.bfloat16)


def local(activations, gate_pre, hidden_grad, up_weights):
    single = jnp.float32
    width = gate_pre.shape[2]
    m = lax.axis_index("mp").astype(jnp.int32)
    d = lax.axis_index("dp").astype(jnp.int32)
    x = lax.rem(lax.axis_index("tensor").astype(jnp.int32), N_X)
    rows = up_weights.shape[1] // N_MP

    parity = lax.rem(lax.axis_index("tensor").astype(jnp.int32) // N_X, 2)
    place = jnp.stack([m, x, parity])
    first_row, first_size = CHUNKS[0]
    first_block = first_row // first_size
    half_blocks = rows // first_size
    piece_shape = jax.ShapeDtypeStruct((N_DP, 128, LEN), jnp.bfloat16)
    half_shape = (HALF, 128, LEN)
    other_x, w_first = pl.pallas_call(
        piece_kernel,
        out_shape=(
            jax.ShapeDtypeStruct(half_shape, jnp.bfloat16),
            jax.ShapeDtypeStruct((first_size, width), jnp.bfloat16),
        ),
        grid_spec=pltpu.PrefetchScalarGridSpec(
            num_scalar_prefetch=1,
            grid=(1,),
            in_specs=[
                pl.BlockSpec(
                    (LEN, 128),
                    lambda i, w, d=d: (0, ((w[2] * HALF + d) * N_MP + 1 - w[0]) * N_X + w[1]),
                )
                for d in range(HALF)
            ]
            + [
                pl.BlockSpec(
                    (first_size, width), lambda i, w: ((1 - w[0]) * half_blocks + first_block, 0)
                )
            ],
            out_specs=[
                pl.BlockSpec(half_shape, lambda i, w: (0, 0, 0)),
                pl.BlockSpec((first_size, width), lambda i, w: (0, 0)),
            ],
        ),
        compiler_params=pltpu.CompilerParams(vmem_limit_bytes=PREP_VMEM_LIMIT),
        cost_estimate=pl.CostEstimate(flops=10**5, bytes_accessed=10**6, transcendentals=0),
        name="pieces",
    )(place, *[activations[0]] * HALF, up_weights[0])

    copies = 4
    still = lambda i, w: (0, 0)
    own_x, cot, part = pl.pallas_call(
        prep_kernel,
        out_shape=(
            piece_shape,
            jax.ShapeDtypeStruct((LEN, width), jnp.bfloat16),
            jax.ShapeDtypeStruct((N_Z_ALL, 1, 128), single),
        ),
        grid_spec=pltpu.PrefetchScalarGridSpec(
            num_scalar_prefetch=1,
            grid=(1,),
            in_specs=[
                pl.BlockSpec(memory_space=pl.ANY),
                pl.BlockSpec((LEN, width), still),
                pl.BlockSpec((LEN, width), still),
            ],
            out_specs=[
                pl.BlockSpec((N_DP, 128, LEN), lambda i, w: (0, 0, 0)),
                pl.BlockSpec((LEN, width), still),
                pl.BlockSpec((N_Z_ALL, 1, 128), lambda i, w: (0, 0, 0)),
            ],
            scratch_shapes=[
                pltpu.VMEM((copies, LEN, D // copies), jnp.bfloat16),
                pltpu.SemaphoreType.DMA((copies,)),
            ],
        ),
        compiler_params=pltpu.CompilerParams(vmem_limit_bytes=PREP_VMEM_LIMIT),
        cost_estimate=pl.CostEstimate(flops=4 * 10**8, bytes_accessed=4 * 10**6, transcendentals=0),
        name="prep",
    )(place, activations[0], gate_pre[0], hidden_grad[0])
    cot_other = lax.ppermute(cot, "mp", MP_SWAP)

    from_other = lax.ppermute(other_x, "mp", MP_SWAP)
    parts = exchange(part, ("mp", "tensor"), Z_GROUPS)
    swapped = lax.ppermute(from_other, "tensor", Z_SWAP)
    packed = pl.pallas_call(
        pack_kernel,
        out_shape=jax.ShapeDtypeStruct((N_DP, 2, 128 + TAIL, LEN), jnp.bfloat16),
        grid_spec=pltpu.PrefetchScalarGridSpec(
            num_scalar_prefetch=1,
            grid=(1,),
            in_specs=[
                pl.BlockSpec((N_DP, 128, LEN), lambda i, w: (0, 0, 0)),
                pl.BlockSpec(half_shape, lambda i, w: (0, 0, 0)),
                pl.BlockSpec(half_shape, lambda i, w: (0, 0, 0)),
                pl.BlockSpec((N_Z_ALL, 1, 128), lambda i, w: (0, 0, 0)),
            ],
            out_specs=pl.BlockSpec((N_DP, 2, 128 + TAIL, LEN), lambda i, w: (0, 0, 0, 0)),
        ),
        compiler_params=pltpu.CompilerParams(vmem_limit_bytes=VMEM_LIMIT),
        cost_estimate=pl.CostEstimate(flops=10**5, bytes_accessed=10**6, transcendentals=0),
        name="pack",
    )(place, own_x, from_other, swapped, parts)
    x_pieces = exchange(packed, "dp")
    x_all = [x_pieces] + [lax.ppermute(x_pieces, "tensor", x_shift(k)) for k in (1, -1, 2)]
    x_from = [x, lax.rem(x + 3, 4), lax.rem(x + 1, 4), lax.rem(x + 2, 4)]

    w_later, _ = lax.optimization_barrier((up_weights[0], cot))
    w_other = []
    for k, (begin, size) in enumerate(CHUNKS):
        piece = w_first
        if k:
            piece = lax.dynamic_slice(w_later, ((1 - m) * rows + begin, 0), (size, width))
        w_other.append(lax.ppermute(piece, "mp", MP_SWAP))

    y = d // N_CORE
    c = lax.rem(d, N_CORE)
    cots, seqs = [], []
    for value in (cot, cot_other):
        pieces = [value] + [lax.ppermute(value, "dp", y_shift(k)) for k in (1, -1, 2)]
        pieces += [lax.ppermute(piece, "dp", CORE_SWAP) for piece in pieces]
        cots += pieces
    for core in (c, 1 - c):
        for shift in (0, 3, 1, 2):
            seqs.append(lax.rem(y + shift, N_Y) * N_CORE + core)

    tile = 256
    n_seq = N_DP
    where = jnp.stack(x_from + seqs).astype(jnp.int32)
    whole = pl.BlockSpec((N_DP, 2, 128 + TAIL, LEN), lambda i, *_: (0, 0, 0, 0))
    a, b = pl.pallas_call(
        functools.partial(fisher_kernel, n_seq),
        out_shape=(
            jax.ShapeDtypeStruct((rows, width), single),
            jax.ShapeDtypeStruct((rows, width), single),
        ),
        grid_spec=pltpu.PrefetchScalarGridSpec(
            num_scalar_prefetch=1,
            grid=(width // tile,),
            in_specs=[whole] * N_X
            + [pl.BlockSpec((LEN, tile), lambda i, *_: (0, i))] * (2 * n_seq)
            + [pl.BlockSpec((rows, tile), lambda i, w: (w[N_X + n_seq], i))],
            out_specs=[pl.BlockSpec((rows, tile), lambda i, *_: (0, i))] * 2,
            scratch_shapes=[
                pltpu.VMEM((2, n_seq, rows, LEN), jnp.bfloat16),
                pltpu.VMEM((2, n_seq, 8, tile), single),
            ],
        ),
        compiler_params=pltpu.CompilerParams(vmem_limit_bytes=VMEM_LIMIT),
        cost_estimate=pl.CostEstimate(flops=4 * 10**9, bytes_accessed=18 * 10**6, transcendentals=0),
        name="fisher",
    )(jnp.concatenate([where, m[None]]), *x_all, *cots, up_weights[0])

    out = None
    for k, (begin, chunk) in enumerate(CHUNKS):
        half = lambda i, k=begin // chunk: (k, 0)
        first = lambda i: (0, 0)
        in_specs = [pl.BlockSpec((chunk, width), half)] * 2 + [pl.BlockSpec((chunk, width), first)]
        operands = [a, b, w_other[k]]
        aliases = {}
        if out is not None:
            in_specs.append(pl.BlockSpec(memory_space=pl.ANY))
            operands.append(out)
            aliases = {3: 0}
        out = pl.pallas_call(
            merge_kernel,
            out_shape=jax.ShapeDtypeStruct((rows, width), jnp.bfloat16),
            grid=(1,),
            in_specs=in_specs,
            out_specs=pl.BlockSpec((chunk, width), half),
            input_output_aliases=aliases,
            compiler_params=pltpu.CompilerParams(vmem_limit_bytes=VMEM_LIMIT),
            cost_estimate=pl.CostEstimate(
                flops=chunk * width * 2, bytes_accessed=chunk * width * 12, transcendentals=0
            ),
        )(*operands)
    return out


def solution(mesh):
    placed = (
        P("mp", "dp", None),
        P("mp", "dp", "tensor"),
        P("mp", "dp", "tensor"),
        P("mp", "dp", "tensor"),
    )

    return jax.shard_map(
        local, mesh=mesh, in_specs=placed, out_specs=P(("dp", "mp"), "tensor"), check_vma=False
    )
```

time: 190 us -> 185 us (0.974)
  starting transfers between devices: 53.9 us -> 36.1 us
  blocking collectives: 0 us -> 15.3 us
  Pallas kernels: 23.4 us -> 32 us
  waiting for transfers between devices: 95.3 us -> 87.6 us
    ppermute x1, waiting for transfers between devices: 21.9 us -> 0.01 us  [local(): from_other = lax.ppermute(other_x, 'mp', MP_SWAP)]
    ppermute x0 -> x1, waiting for transfers between devices: none -> 17.3 us  [local(): swapped = lax.ppermute(from_other, 'tensor', Z_SWAP)]
    all_to_all x3 -> x1, waiting for transfers between devices: 20.9 us -> 5.3 us  [exchange(): lax.all_to_all(value, axis, 0, 0, axis_index_groups=groups, tiled=True)]
    all_to_all x0 -> x1, blocking collectives: none -> 15.3 us  [exchange(): lax.all_to_all(value, axis, 0, 0, axis_index_groups=groups, tiled=True)]
    all_to_all x3 -> x1, starting transfers between devices: 18 us -> 4.47 us  [exchange(): lax.all_to_all(value, axis, 0, 0, axis_index_groups=groups, tiled=True)]
    ppermute x6, waiting for transfers between devices: 4.91 us -> 17.1 us  [local(): lax.ppermute(value, 'dp', y_shift(k))]
    pallas_call x1 -> x3, Pallas kernels: 1.5 us -> 9.28 us  [the longest x1 5.13 us: local(): pl.pallas_call(prep_kernel, out_shape=(piece_shape, jax.ShapeDtypeStruct(...]
    ppermute x1, starting transfers between devices: 6.38 us -> 0.09 us  [local(): cot_other = lax.ppermute(cot, 'mp', MP_SWAP)]
  transfers between devices with their start and end apart: 26 -> 25, of which waited for: 11 -> 8; matrix products, arithmetic and copies ran while one was open for 3% -> 2% of each run, Pallas kernels for 11% -> 15%
where the time goes in v2:
time: 185 us; the launch traced here: 182 us
  waiting for transfers between devices  87.6 us (47%)
  starting transfers between devices  36.1 us (20%)
  Pallas kernels  32 us (17%)
  blocking collectives  15.3 us (8%)
  local copies, waits for them, and re-layouts  10.3 us (6%)
    ppermute x4, waiting for transfers between devices, local(): w_other.append(lax.ppermute(piece, 'mp', MP_SWAP))  36.3 us
    ppermute x1, waiting for transfers between devices, local(): swapped = lax.ppermute(from_other, 'tensor', Z_SWAP)  17.3 us
    ppermute x6, waiting for transfers between devices, local(): lax.ppermute(value, 'dp', y_shift(k))  17.1 us
    all_to_all x1, blocking collectives, exchange(): lax.all_to_all(value, axis, 0, 0, axis_index_groups=groups, tiled=True)  15.3 us
    pallas_call x1, Pallas kernels, local(): pl.pallas_call(functools.partial(fisher_kernel, n_seq), out_shape=(jax.Sh...  13.8 us
    ppermute x3, waiting for transfers between devices, local(): lax.ppermute(x_pieces, 'tensor', x_shift(k))  11.5 us
    ppermute x6, starting transfers between devices, local(): lax.ppermute(value, 'dp', y_shift(k))  10.2 us
    ppermute x4, starting transfers between devices, local(): w_other.append(lax.ppermute(piece, 'mp', MP_SWAP))  9.11 us
  transfers between devices with their start and end apart: 25, of which 8 were waited for; matrix products, arithmetic and copies ran while one was open for 2% of the time, Pallas kernels for 15%

profile of v2, /device:TPU:38, one launch (start us, length us, event | category | flops | bytes accessed | tf_op | source)
XLA Modules:
  0.0 182.1 jit_solution(11189388243636670380)
XLA Ops:
  0.7 2.8 %pieces.1 = (bf16[4,128,128]{2,1,0:T(8,128)(2,1)}, bf16[128,1792]{1,0:T(8,128)(2,1)}) custom-call(s32[3]{0:T(128)} %pad_add_fusion.where, bf16[128,8192]{1,0:T(8,128)(2,1)} %bitcast.18, bf16[128,8192]{1,0:T(8,128)(2,1)} %bitcast.19, bf16[128,8192]{1,0:T(8,128)(2,1)} %bitcast.20, bf16[128,8192]{1,0:T(8,128)(2,1)} %bitcast.21, bf16[1024,1792]{1,0:T(8,128)(2,1)} %bitcast.23), custom_call_target="tpu_custom_call" | custom-call | flops 100000 | bytes 1000000 | tf_op jit(solution)/shard_map/pieces/pallas_call | solution.py:176
  3.4 6.3 %collective-permute-start = (bf16[4,128,128]{2,1,0:T(8,128)(2,1)}, bf16[4,128,128]{2,1,0:T(8,128)(2,1)S(1)}, u32[]{:S(2)}, u32[]{:S(2)}) collective-permute-start(bf16[4,128,128]{2,1,0:T(8,128)(2,1)} %get-tuple-element.14), channel_id=1, source_target_pairs={{0,128},{128,0},{1,129},{129,1},{2,130},{130,2},{3,131},{131,3},{4... | collective-permute-start | bytes 393224 | tf_op jit(solution)/shard_map/ppermute | solution.py:240
  9.7 5.1 %prep.1 = (bf16[8,128,128]{2,1,0:T(8,128)(2,1)}, bf16[128,1792]{1,0:T(8,128)(2,1)}, f32[8,1,128]{2,1,0:T(1,128)}) custom-call(s32[3]{0:T(128)} %pad_add_fusion.where, bf16[128,8192]{1,0:T(8,128)(2,1)} %bitcast.22, bf16[128,1792]{1,0:T(8,128)(2,1)} %bitcast.28, bf16[128,1792]{1,0:T(8,128)(2,1)} %bitcast.29), custom_call_target="tpu_custom_call" | custom-call | flops 400000000 | bytes 4000000 | tf_op jit(solution)/shard_map/prep/pallas_call | solution.py:209
  15.0 3.1 %collective-permute-start.6 = (bf16[128,1792]{1,0:T(8,128)(2,1)}, bf16[128,1792]{1,0:T(8,128)(2,1)S(1)}, u32[]{:S(2)}, u32[]{:S(2)}) collective-permute-start(bf16[128,1792]{1,0:T(8,128)(2,1)} %get-tuple-element.16.refs_4_), channel_id=1, source_target_pairs={{0,96},{16,112},{32,0},{48,16},{64,32},{80,48},{96,64},{112,80},{1... | collective-permute-start | bytes 1376264 | tf_op jit(solution)/shard_map/ppermute | solution.py:277
  20.7 17.3 %collective-permute-done.1.swapped_ref = bf16[4,128,128]{2,1,0:T(8,128)(2,1)S(1)} collective-permute-done((bf16[4,128,128]{2,1,0:T(8,128)(2,1)S(1)}, bf16[4,128,128]{2,1,0:T(8,128)(2,1)S(1)}, u32[]{:S(2)}, u32[]{:S(2)}) %collective-permute-start.1) | collective-permute-done | bytes 131104 | tf_op jit(solution)/shard_map/ppermute | solution.py:242
  38.0 15.3 %all_to_all.10.part_ref = f32[8,1,128]{2,1,0:T(1,128)S(1)} all-to-all(f32[8,1,128]{2,1,0:T(1,128)} %get-tuple-element.15), channel_id=1, replica_groups={{0,4,8,12,128,132,136,140},{1,5,9,13,129,133,137,141},{2,6,10,14,130,13..., dimensions={0} | all-to-all | bytes 8192 | tf_op jit(solution)/shard_map/all_to_all | solution.py:38
  55.6 4.5 %all-to-all-start.1 = ((bf16[8,2,136,128]{3,2,1,0:T(8,128)(2,1)}), bf16[8,2,136,128]{3,2,1,0:T(8,128)(2,1)}, u32[]{:S(2)}, u32[]{:S(2)}) async-start(bf16[8,2,136,128]{3,2,1,0:T(8,128)(2,1)} %pack.1), calls=%async_computation.1 | async-start | bytes 1114112 | tf_op jit(solution)/shard_map/all_to_all | solution.py:38
  60.1 2.0 %collective-permute-start.13 = (bf16[128,1792]{1,0:T(8,128)(2,1)}, bf16[128,1792]{1,0:T(8,128)(2,1)}, u32[]{:S(2)}, u32[]{:S(2)}) collective-permute-start(bf16[128,1792]{1,0:T(8,128)(2,1)} %collective-permute-done.12.refs_12_), channel_id=1, source_target_pairs={{0,32},{16,48},{32,64},{48,80},{64,96},{80,112},{96,0},{112,16},{1... | collective-permute-start | bytes 1376264 | tf_op jit(solution)/shard_map/ppermute | solution.py:277
  63.4 2.2 %collective-permute-start.15 = (bf16[128,1792]{1,0:T(8,128)(2,1)}, bf16[128,1792]{1,0:T(8,128)(2,1)}, u32[]{:S(2)}, u32[]{:S(2)}) collective-permute-start(bf16[128,1792]{1,0:T(8,128)(2,1)} %collective-permute-done.12.refs_12_), channel_id=1, source_target_pairs={{0,64},{16,80},{32,96},{48,112},{64,0},{80,16},{96,32},{112,48},{1... | collective-permute-start | bytes 1376264 | tf_op jit(solution)/shard_map/ppermute | solution.py:277
  66.1 5.3 %all-to-all-done.1.refs_0_ = bf16[8,2,136,128]{3,2,1,0:T(8,128)(2,1)} async-done(((bf16[8,2,136,128]{3,2,1,0:T(8,128)(2,1)}), bf16[8,2,136,128]{3,2,1,0:T(8,128)(2,1)}, u32[]{:S(2)}, u32[]{:S(2)}) %all-to-all-start.1) | async-done | bytes 557088 | tf_op jit(solution)/shard_map/all_to_all | solution.py:38
  71.4 9.2 %collective-permute-done.13.refs_13_ = bf16[128,1792]{1,0:T(8,128)(2,1)} collective-permute-done((bf16[128,1792]{1,0:T(8,128)(2,1)}, bf16[128,1792]{1,0:T(8,128)(2,1)}, u32[]{:S(2)}, u32[]{:S(2)}) %collective-permute-start.13) | collective-permute-done | bytes 458784 | tf_op jit(solution)/shard_map/ppermute | solution.py:277
  81.1 1.6 collective-permute-start.3
  82.6 7.9 %collective-permute-done.15.refs_15_ = bf16[128,1792]{1,0:T(8,128)(2,1)} collective-permute-done((bf16[128,1792]{1,0:T(8,128)(2,1)}, bf16[128,1792]{1,0:T(8,128)(2,1)}, u32[]{:S(2)}, u32[]{:S(2)}) %collective-permute-start.15) | collective-permute-done | bytes 458784 | tf_op jit(solution)/shard_map/ppermute | solution.py:277
  92.5 2.3 %constant_dynamic-slice_fusion = bf16[256,1792]{1,0:T(8,128)(2,1)} fusion(bf16[1024,1792]{1,0:T(8,128)(2,1)} %bitcast.24, s32[]{:T(128)S(6)} %select_n.21), kind=kLoop, calls=%fused_computation | loop fusion | bytes 1835012 | tf_op jit(solution)/shard_map/dynamic_slice | solution.py:270
  96.8 11.5 %collective-permute-done.3.refs_2_ = bf16[8,2,136,128]{3,2,1,0:T(8,128)(2,1)} collective-permute-done((bf16[8,2,136,128]{3,2,1,0:T(8,128)(2,1)}, bf16[8,2,136,128]{3,2,1,0:T(8,128)(2,1)}, u32[]{:S(2)}, u32[]{:S(2)}) %collective-permute-start.3) | collective-permute-done | bytes 557088 | tf_op jit(solution)/shard_map/ppermute | solution.py:262
  111.9 4.6 %collective-permute-start.21 = (bf16[96,1792]{1,0:T(8,128)(2,1)S(1)}, bf16[96,1792]{1,0:T(8,128)(2,1)S(1)}, u32[]{:S(2)}, u32[]{:S(2)}) collective-permute-start(bf16[96,1792]{1,0:T(8,128)(2,1)S(1)} %constant_dynamic-slice_fusion.1), channel_id=1, source_target_pairs={{0,128},{128,0},{1,129},{129,1},{2,130},{130,2},{3,131},{131,3},{4... | collective-permute-start | bytes 1032200 | tf_op jit(solution)/shard_map/ppermute | solution.py:271
  120.9 13.8 %fisher.1 = (f32[512,1792]{1,0:T(8,128)}, f32[512,1792]{1,0:T(8,128)}) custom-call(s32[13]{0:T(128)S(1)} %concatenate.3.where, bf16[8,2,136,128]{3,2,1,0:T(8,128)(2,1)} %all-to-all-done.1.refs_0_, bf16[8,2,136,128]{3,2,1,0:T(8,128)(2,1)} %collective-permute-done.2.refs_1_, bf16[8,2,136,128]{3,2,1,0:T(8,128)(2,1)} %collective-permute-done.3.refs_2_, ...), custom_call_target="tpu_custom_call" | custom-call | flops 4000000000 | bytes 18000000 | tf_op jit(solution)/shard_map/fisher/pallas_call | solution.py:288
  134.8 32.5 %collective-permute-done.23.w_ref = bf16[128,1792]{1,0:T(8,128)(2,1)S(1)} collective-permute-done((bf16[128,1792]{1,0:T(8,128)(2,1)}, bf16[128,1792]{1,0:T(8,128)(2,1)S(1)}, u32[]{:S(2)}, u32[]{:S(2)}) %collective-permute-start.23) | collective-permute-done | bytes 458784 | tf_op jit(solution)/shard_map/ppermute | solution.py:271
  167.3 2.0 %copy-done = f32[512,1792]{1,0:T(8,128)S(1)} copy-done((f32[512,1792]{1,0:T(8,128)S(1)}, f32[512,1792]{1,0:T(8,128)}, u32[]{:S(2)}) %copy-start) | copy-done | bytes 3670040
  169.4 2.1 %shard_map.46.refs_0_ = bf16[512,1792]{1,0:T(8,128)(2,1)} custom-call(f32[512,1792]{1,0:T(8,128)S(1)} %copy-done, f32[512,1792]{1,0:T(8,128)} %get-tuple-element.18.b_ref, bf16[128,1792]{1,0:T(8,128)(2,1)S(1)} %collective-permute-done.23.w_ref), custom_call_target="tpu_custom_call" | custom-call | flops 458752 | bytes 2752512 | tf_op jit(solution)/shard_map/pallas_call | solution.py:322
  171.4 3.3 %shard_map.47.refs_0_ = bf16[512,1792]{1,0:T(8,128)(2,1)} custom-call(f32[512,1792]{1,0:T(8,128)} %get-tuple-element.17.a_ref, f32[512,1792]{1,0:T(8,128)} %get-tuple-element.18.b_ref, bf16[256,1792]{1,0:T(8,128)(2,1)S(1)} %collective-permute-done.22.w_ref, bf16[512,1792]{1,0:T(8,128)(2,1)} %shard_map.46.refs_0_), custom_call_target="tpu_custom_call", output_to_operand_aliasing={{}: (3, {})} | custom-call | flops 917504 | bytes 5505024 | tf_op jit(solution)/shard_map/pallas_call | solution.py:322
  174.8 3.4 %collective-permute-done.21.w_ref = bf16[96,1792]{1,0:T(8,128)(2,1)S(1)} collective-permute-done((bf16[96,1792]{1,0:T(8,128)(2,1)S(1)}, bf16[96,1792]{1,0:T(8,128)(2,1)S(1)}, u32[]{:S(2)}, u32[]{:S(2)}) %collective-permute-start.21) | collective-permute-done | bytes 344096 | tf_op jit(solution)/shard_map/ppermute | solution.py:271
  178.1 1.9 %shard_map.48.refs_0_ = bf16[512,1792]{1,0:T(8,128)(2,1)} custom-call(f32[512,1792]{1,0:T(8,128)S(1)} %copy-done.1, f32[512,1792]{1,0:T(8,128)} %get-tuple-element.18.b_ref, bf16[96,1792]{1,0:T(8,128)(2,1)S(1)} %collective-permute-done.21.w_ref, bf16[512,1792]{1,0:T(8,128)(2,1)} %shard_map.47.refs_0_), custom_call_target="tpu_custom_call", output_to_operand_aliasing={{}: (3, {})} | custom-call | flops 344064 | bytes 2064384 | tf_op jit(solution)/shard_map/pallas_call | solution.py:322
  180.5 1.6 shard_map.49
  (62 shorter events, 20.5 us)
Async XLA Ops:
  3.4 16.2 %collective-permute-start = (bf16[4,128,128]{2,1,0:T(8,128)(2,1)}, bf16[4,128,128]{2,1,0:T(8,128)(2,1)S(1)}, u32[]{:S(2)}, u32[]{:S(2)}) collective-permute-start(bf16[4,128,128]{2,1,0:T(8,128)(2,1)} %get-tuple-element.14), channel_id=1, source_target_pairs={{0,128},{128,0},{1,129},{129,1},{2,130},{130,2},{3,131},{131,3},{4... | collective-permute-start | bytes 393224 | tf_op jit(solution)/shard_map/ppermute | solution.py:240
  14.9 45.2 %collective-permute-start.12 = (bf16[128,1792]{1,0:T(8,128)(2,1)}, bf16[128,1792]{1,0:T(8,128)(2,1)}, u32[]{:S(2)}, u32[]{:S(2)}) collective-permute-start(bf16[128,1792]{1,0:T(8,128)(2,1)} %get-tuple-element.16.refs_4_), channel_id=1, source_target_pairs={{0,128},{128,0},{1,129},{129,1},{2,130},{130,2},{3,131},{131,3},{4... | collective-permute-start | bytes 1376264 | tf_op jit(solution)/shard_map/ppermute | solution.py:238
  15.0 47.1 %collective-permute-start.6 = (bf16[128,1792]{1,0:T(8,128)(2,1)}, bf16[128,1792]{1,0:T(8,128)(2,1)S(1)}, u32[]{:S(2)}, u32[]{:S(2)}) collective-permute-start(bf16[128,1792]{1,0:T(8,128)(2,1)} %get-tuple-element.16.refs_4_), channel_id=1, source_target_pairs={{0,96},{16,112},{32,0},{48,16},{64,32},{80,48},{96,64},{112,80},{1... | collective-permute-start | bytes 1376264 | tf_op jit(solution)/shard_map/ppermute | solution.py:277
  18.0 45.3 %collective-permute-start.7 = (bf16[128,1792]{1,0:T(8,128)(2,1)}, bf16[128,1792]{1,0:T(8,128)(2,1)S(1)}, u32[]{:S(2)}, u32[]{:S(2)}) collective-permute-start(bf16[128,1792]{1,0:T(8,128)(2,1)} %get-tuple-element.16.refs_4_), channel_id=1, source_target_pairs={{0,64},{16,80},{32,96},{48,112},{64,0},{80,16},{96,32},{112,48},{1... | collective-permute-start | bytes 1376264 | tf_op jit(solution)/shard_map/ppermute | solution.py:277
  18.7 46.9 %collective-permute-start.5 = (bf16[128,1792]{1,0:T(8,128)(2,1)}, bf16[128,1792]{1,0:T(8,128)(2,1)S(1)}, u32[]{:S(2)}, u32[]{:S(2)}) collective-permute-start(bf16[128,1792]{1,0:T(8,128)(2,1)} %get-tuple-element.16.refs_4_), channel_id=1, source_target_pairs={{0,32},{16,48},{32,64},{48,80},{64,96},{80,112},{96,0},{112,16},{1... | collective-permute-start | bytes 1376264 | tf_op jit(solution)/shard_map/ppermute | solution.py:277
  19.6 18.3 %collective-permute-start.1 = (bf16[4,128,128]{2,1,0:T(8,128)(2,1)S(1)}, bf16[4,128,128]{2,1,0:T(8,128)(2,1)S(1)}, u32[]{:S(2)}, u32[]{:S(2)}) collective-permute-start(bf16[4,128,128]{2,1,0:T(8,128)(2,1)S(1)} %collective-permute-done.kept_ref), channel_id=1, source_target_pairs={{0,4},{1,5},{2,6},{3,7},{4,0},{5,1},{6,2},{7,3},{8,12},{9,13},{10,... | collective-permute-start | bytes 393224 | tf_op jit(solution)/shard_map/ppermute | solution.py:242
  38.0 27.7 %collective-permute-start.8 = (bf16[128,1792]{1,0:T(8,128)(2,1)}, bf16[128,1792]{1,0:T(8,128)(2,1)S(1)}, u32[]{:S(2)}, u32[]{:S(2)}) collective-permute-start(bf16[128,1792]{1,0:T(8,128)(2,1)} %get-tuple-element.16.refs_4_), channel_id=1, source_target_pairs={{0,16},{16,0},{32,48},{48,32},{64,80},{80,64},{96,112},{112,96},{1... | collective-permute-start | bytes 1376264 | tf_op jit(solution)/shard_map/ppermute | solution.py:278
  55.6 15.9 %all-to-all-start.1 = ((bf16[8,2,136,128]{3,2,1,0:T(8,128)(2,1)}), bf16[8,2,136,128]{3,2,1,0:T(8,128)(2,1)}, u32[]{:S(2)}, u32[]{:S(2)}) async-start(bf16[8,2,136,128]{3,2,1,0:T(8,128)(2,1)} %pack.1), calls=%async_computation.1 | async-start | bytes 1114112 | tf_op jit(solution)/shard_map/all_to_all | solution.py:38
  60.1 20.5 %collective-permute-start.13 = (bf16[128,1792]{1,0:T(8,128)(2,1)}, bf16[128,1792]{1,0:T(8,128)(2,1)}, u32[]{:S(2)}, u32[]{:S(2)}) collective-permute-start(bf16[128,1792]{1,0:T(8,128)(2,1)} %collective-permute-done.12.refs_12_), channel_id=1, source_target_pairs={{0,32},{16,48},{32,64},{48,80},{64,96},{80,112},{96,0},{112,16},{1... | collective-permute-start | bytes 1376264 | tf_op jit(solution)/shard_map/ppermute | solution.py:277
  62.1 19.0 %collective-permute-start.14 = (bf16[128,1792]{1,0:T(8,128)(2,1)}, bf16[128,1792]{1,0:T(8,128)(2,1)}, u32[]{:S(2)}, u32[]{:S(2)}) collective-permute-start(bf16[128,1792]{1,0:T(8,128)(2,1)} %collective-permute-done.12.refs_12_), channel_id=1, source_target_pairs={{0,96},{16,112},{32,0},{48,16},{64,32},{80,48},{96,64},{112,80},{1... | collective-permute-start | bytes 1376264 | tf_op jit(solution)/shard_map/ppermute | solution.py:277
  63.4 27.1 %collective-permute-start.15 = (bf16[128,1792]{1,0:T(8,128)(2,1)}, bf16[128,1792]{1,0:T(8,128)(2,1)}, u32[]{:S(2)}, u32[]{:S(2)}) collective-permute-start(bf16[128,1792]{1,0:T(8,128)(2,1)} %collective-permute-done.12.refs_12_), channel_id=1, source_target_pairs={{0,64},{16,80},{32,96},{48,112},{64,0},{80,16},{96,32},{112,48},{1... | collective-permute-start | bytes 1376264 | tf_op jit(solution)/shard_map/ppermute | solution.py:277
  65.6 24.9 %collective-permute-start.10 = (bf16[128,1792]{1,0:T(8,128)(2,1)S(1)}, bf16[128,1792]{1,0:T(8,128)(2,1)S(1)}, u32[]{:S(2)}, u32[]{:S(2)}) collective-permute-start(bf16[128,1792]{1,0:T(8,128)(2,1)S(1)} %collective-permute-done.6.refs_6_), channel_id=1, source_target_pairs={{0,16},{16,0},{32,48},{48,32},{64,80},{80,64},{96,112},{112,96},{1... | collective-permute-start | bytes 1376264 | tf_op jit(solution)/shard_map/ppermute | solution.py:278
  65.6 25.4 %collective-permute-start.11 = (bf16[128,1792]{1,0:T(8,128)(2,1)S(1)}, bf16[128,1792]{1,0:T(8,128)(2,1)}, u32[]{:S(2)}, u32[]{:S(2)}) collective-permute-start(bf16[128,1792]{1,0:T(8,128)(2,1)S(1)} %collective-permute-done.7.refs_7_), channel_id=1, source_target_pairs={{0,16},{16,0},{32,48},{48,32},{64,80},{80,64},{96,112},{112,96},{1... | collective-permute-start | bytes 1376264 | tf_op jit(solution)/shard_map/ppermute | solution.py:278
  80.6 15.7 %collective-permute-start.2 = (bf16[8,2,136,128]{3,2,1,0:T(8,128)(2,1)}, bf16[8,2,136,128]{3,2,1,0:T(8,128)(2,1)}, u32[]{:S(2)}, u32[]{:S(2)}) collective-permute-start(bf16[8,2,136,128]{3,2,1,0:T(8,128)(2,1)} %all-to-all-done.1.refs_0_), channel_id=1, source_target_pairs={{0,1},{1,2},{2,3},{3,0},{4,5},{5,6},{6,7},{7,4},{8,9},{9,10},{10,1... | collective-permute-start | bytes 1671176 | tf_op jit(solution)/shard_map/ppermute | solution.py:262
  81.1 27.2 %collective-permute-start.3 = (bf16[8,2,136,128]{3,2,1,0:T(8,128)(2,1)}, bf16[8,2,136,128]{3,2,1,0:T(8,128)(2,1)}, u32[]{:S(2)}, u32[]{:S(2)}) collective-permute-start(bf16[8,2,136,128]{3,2,1,0:T(8,128)(2,1)} %all-to-all-done.1.refs_0_), channel_id=1, source_target_pairs={{0,3},{1,0},{2,1},{3,2},{4,7},{5,4},{6,5},{7,6},{8,11},{9,8},{10,9... | collective-permute-start | bytes 1671176 | tf_op jit(solution)/shard_map/ppermute | solution.py:262
  90.5 5.7 %collective-permute-start.9 = (bf16[128,1792]{1,0:T(8,128)(2,1)S(1)}, bf16[128,1792]{1,0:T(8,128)(2,1)}, u32[]{:S(2)}, u32[]{:S(2)}) collective-permute-start(bf16[128,1792]{1,0:T(8,128)(2,1)S(1)} %collective-permute-done.5.refs_5_), channel_id=1, source_target_pairs={{0,16},{16,0},{32,48},{48,32},{64,80},{80,64},{96,112},{112,96},{1... | collective-permute-start | bytes 1376264 | tf_op jit(solution)/shard_map/ppermute | solution.py:278
  91.1 18.2 %collective-permute-start.4 = (bf16[8,2,136,128]{3,2,1,0:T(8,128)(2,1)}, bf16[8,2,136,128]{3,2,1,0:T(8,128)(2,1)}, u32[]{:S(2)}, u32[]{:S(2)}) collective-permute-start(bf16[8,2,136,128]{3,2,1,0:T(8,128)(2,1)} %all-to-all-done.1.refs_0_), channel_id=1, source_target_pairs={{0,2},{1,3},{2,0},{3,1},{4,6},{5,7},{6,4},{7,5},{8,10},{9,11},{10,... | collective-permute-start | bytes 1671176 | tf_op jit(solution)/shard_map/ppermute | solution.py:262
  94.7 76.7 %collective-permute-start.22 = (bf16[256,1792]{1,0:T(8,128)(2,1)}, bf16[256,1792]{1,0:T(8,128)(2,1)S(1)}, u32[]{:S(2)}, u32[]{:S(2)}) collective-permute-start(bf16[256,1792]{1,0:T(8,128)(2,1)} %constant_dynamic-slice_fusion), channel_id=1, source_target_pairs={{0,128},{128,0},{1,129},{129,1},{2,130},{130,2},{3,131},{131,3},{4... | collective-permute-start | bytes 2752520 | tf_op jit(solution)/shard_map/ppermute | solution.py:271
  96.3 15.6 %collective-permute-start.17 = (bf16[128,1792]{1,0:T(8,128)(2,1)}, bf16[128,1792]{1,0:T(8,128)(2,1)}, u32[]{:S(2)}, u32[]{:S(2)}) collective-permute-start(bf16[128,1792]{1,0:T(8,128)(2,1)} %collective-permute-done.13.refs_13_), channel_id=1, source_target_pairs={{0,16},{16,0},{32,48},{48,32},{64,80},{80,64},{96,112},{112,96},{1... | collective-permute-start | bytes 1376264 | tf_op jit(solution)/shard_map/ppermute | solution.py:278
  96.3 20.1 %collective-permute-start.18 = (bf16[128,1792]{1,0:T(8,128)(2,1)}, bf16[128,1792]{1,0:T(8,128)(2,1)}, u32[]{:S(2)}, u32[]{:S(2)}) collective-permute-start(bf16[128,1792]{1,0:T(8,128)(2,1)} %collective-permute-done.14.refs_14_), channel_id=1, source_target_pairs={{0,16},{16,0},{32,48},{48,32},{64,80},{80,64},{96,112},{112,96},{1... | collective-permute-start | bytes 1376264 | tf_op jit(solution)/shard_map/ppermute | solution.py:278
  108.3 9.6 %collective-permute-start.19 = (bf16[128,1792]{1,0:T(8,128)(2,1)}, bf16[128,1792]{1,0:T(8,128)(2,1)}, u32[]{:S(2)}, u32[]{:S(2)}) collective-permute-start(bf16[128,1792]{1,0:T(8,128)(2,1)} %collective-permute-done.15.refs_15_), channel_id=1, source_target_pairs={{0,16},{16,0},{32,48},{48,32},{64,80},{80,64},{96,112},{112,96},{1... | collective-permute-start | bytes 1376264 | tf_op jit(solution)/shard_map/ppermute | solution.py:278
  109.3 58.0 %collective-permute-start.23 = (bf16[128,1792]{1,0:T(8,128)(2,1)}, bf16[128,1792]{1,0:T(8,128)(2,1)S(1)}, u32[]{:S(2)}, u32[]{:S(2)}) collective-permute-start(bf16[128,1792]{1,0:T(8,128)(2,1)} %get-tuple-element.20), channel_id=1, source_target_pairs={{0,128},{128,0},{1,129},{129,1},{2,130},{130,2},{3,131},{131,3},{4... | collective-permute-start | bytes 1376264 | tf_op jit(solution)/shard_map/ppermute | solution.py:271
  111.9 66.3 %collective-permute-start.21 = (bf16[96,1792]{1,0:T(8,128)(2,1)S(1)}, bf16[96,1792]{1,0:T(8,128)(2,1)S(1)}, u32[]{:S(2)}, u32[]{:S(2)}) collective-permute-start(bf16[96,1792]{1,0:T(8,128)(2,1)S(1)} %constant_dynamic-slice_fusion.1), channel_id=1, source_target_pairs={{0,128},{128,0},{1,129},{129,1},{2,130},{130,2},{3,131},{131,3},{4... | collective-permute-start | bytes 1032200 | tf_op jit(solution)/shard_map/ppermute | solution.py:271
  116.4 64.1 %collective-permute-start.20 = (bf16[32,1792]{1,0:T(8,128)(2,1)S(1)}, bf16[32,1792]{1,0:T(8,128)(2,1)S(1)}, u32[]{:S(2)}, u32[]{:S(2)}) collective-permute-start(bf16[32,1792]{1,0:T(8,128)(2,1)S(1)} %constant_dynamic-slice_fusion.2), channel_id=1, source_target_pairs={{0,128},{128,0},{1,129},{129,1},{2,130},{130,2},{3,131},{131,3},{4... | collective-permute-start | bytes 344072 | tf_op jit(solution)/shard_map/ppermute | solution.py:271
  (12 other events, 210.2 us)
